TPU v7x, 256 devices: a whole 4x4x8 slice. The times are simulated.
256 devices in a mesh: ctx: 32 (over z, y), head: 8 (over x, core).
Axes of the slice: x: 4, y: 4, z: 8, core: 2. Of those that a mesh axis runs over, the one named last changes fastest.
Arguments:
- queries: bfloat16 [4096, 8192], P('ctx', 'head'), may hold values from -6 to 6
- key_rows: bfloat16 [4096, 1024], P(('ctx', 'head')), may hold values from -6 to 6
- value_matrix_rows: bfloat16 [4096, 1024], P(('ctx', 'head')), may hold values from -6 to 6
- grad_out: bfloat16 [4096, 8192], P('ctx', 'head'), may hold values from -6 to 6
- doc_ids: int32 [4096], replicated, may hold values from 0 to 3, never falling along the last dimension, each value on 1 to 2048 neighbouring positions
- block_owner: int32 [32, 32], replicated, may hold values from 0 to 31, each once within a row
Outputs:
- attention: bfloat16 [4096, 8192], P('ctx', 'head')
- owned_lse: float32 [64, 4096], P('head', 'ctx')
- grad_query: bfloat16 [4096, 8192], P('ctx', 'head')
- key_gradient: bfloat16 [4096, 1024], P(('ctx', 'head'))
- value_gradient: bfloat16 [4096, 1024], P(('ctx', 'head'))
Inputs may be any that keep to these rules, and one draw needn't show every extreme that they name: `doc_ids`: never falls along the tokens; every document holds 1 to 2048 tokens. `block_owner`: entry [d, i] names the device that owns block i (tokens d * 128 + i * 4 onward, 4 of them) of token shard d; each row names every device once.
All inputs are finite; a program needn't handle non-finite values.
Results may differ from a plain program's by a relative error of at most 0.02.
Values may be sent and summed in bfloat16 or wider, within the bound.
A program may use at most 64 MiB of HBM per device.

v0:
```python
import jax
import jax.numpy as jnp
from jax import lax
from jax.sharding import Mesh
from jax.sharding import PartitionSpec as P

HEAD_SIZE = 128
CTX = ("ctx_0", "ctx_1")
CTX_HEAD = ("ctx_0", "ctx_1", "head")


mask_value = -1e30


def side_by_side(arrays, axis, dim, along):
    both = jnp.concatenate(arrays, axis=along)
    out, at, done = (lax.all_gather(both, axis, axis=dim, tiled=True), 0, [])
    for a in arrays:
        done.append(lax.slice_in_dim(out, at, at + a.shape[along], axis=along))
        at += a.shape[along]
    return tuple(done)


def scatter_axes(value, axes, dim):
    if not axes:
        return value
    nearer = lax.psum_scatter(value, axes[0], scatter_dimension=dim, tiled=True)
    return scatter_axes(nearer, axes[1:], dim)


def tile_mask(query_docs, positions, doc_ids, tile_start, tile_rows):
    key_docs = lax.dynamic_slice_in_dim(doc_ids, tile_start, tile_rows)
    key_places = tile_start + jnp.arange(tile_rows, dtype=jnp.int32)
    return (query_docs[:, None] == key_docs[None, :]) & (key_places[None, :] <= positions[:, None])


def sweep_keys(carried, keys_part, values_part, first_row, tile_fn):
    key_count = keys_part.shape[0]
    tile_rows = 512
    tile_count = key_count // tile_rows

    def advance(running, inputs):
        tile_index, key_tile, value_tile = inputs
        return (tile_fn(running, key_tile, value_tile, first_row + tile_index * tile_rows), None)

    carried, unused = lax.scan(
        advance,
        carried,
        (
            jnp.arange(tile_count, dtype=jnp.int32),
            keys_part.reshape(tile_count, tile_rows, -1),
            values_part.reshape(tile_count, tile_rows, -1),
        ),
    )
    return carried


def body(queries, key_rows, value_matrix_rows, grad_out, doc_ids, block_owner):
    shards = lax.axis_size(CTX)
    shard_index = lax.axis_index(CTX)
    tok_dev = queries.shape[0]
    block_rows = tok_dev // shards
    score_scale = HEAD_SIZE ** (-0.5)
    key_local, value_local = (
        lax.all_to_all(key_rows, "head", split_axis=1, concat_axis=0, tiled=True),
        lax.all_to_all(value_matrix_rows, "head", split_axis=1, concat_axis=0, tiled=True),
    )
    kv_heads = key_local.shape[1] // HEAD_SIZE
    group_size = queries.shape[1] // HEAD_SIZE // kv_heads
    inverse = jnp.argsort(block_owner, axis=1)
    send_order = lax.dynamic_index_in_dim(inverse, shard_index, 0, keepdims=False)
    query_own, grad_own = (queries, grad_out)
    positions = shard_index * tok_dev + jnp.arange(tok_dev, dtype=jnp.int32)
    query_docs = doc_ids[positions]
    grouped = query_own.reshape(tok_dev, kv_heads, group_size, HEAD_SIZE)
    grad_grouped = grad_own.reshape(tok_dev, kv_heads, group_size, HEAD_SIZE)

    def tile_scores(key_tile):
        key_heads = key_tile.reshape(key_tile.shape[0], kv_heads, HEAD_SIZE)
        scores = (
            jnp.einsum("tkgd,skd->kgts", grouped, key_heads, preferred_element_type=jnp.float32)
            * score_scale
        )
        return (scores, key_heads)

    def forward_tile(carried, key_tile, value_tile, tile_start):
        allowed = tile_mask(query_docs, positions, doc_ids, tile_start, key_tile.shape[0])

        def update(running):
            row_max, row_sum, weighted = running
            scores, key_heads = tile_scores(key_tile)
            masked = jnp.where(allowed, scores, mask_value)
            new_max = jnp.maximum(row_max, jnp.max(masked, axis=-1))
            weights_raw = jnp.where(allowed, jnp.exp(masked - new_max[..., None]), 0.0)
            rescale = jnp.exp(row_max - new_max)
            value_heads = value_tile.reshape(value_tile.shape[0], kv_heads, HEAD_SIZE)
            weighted = weighted * rescale[..., None] + jnp.einsum(
                "kgts,skd->kgtd",
                weights_raw.astype(jnp.bfloat16),
                value_heads,
                preferred_element_type=jnp.float32,
            )
            row_sum = row_sum * rescale + jnp.sum(weights_raw, axis=-1)
            return (new_max, row_sum, weighted)

        return lax.cond(jnp.any(allowed), update, lambda running: running, carried)

    initial = (
        jnp.full((kv_heads, group_size, tok_dev), mask_value, jnp.float32),
        jnp.zeros((kv_heads, group_size, tok_dev), jnp.float32),
        jnp.zeros((kv_heads, group_size, tok_dev, HEAD_SIZE), jnp.float32),
    )
    all_keys, all_values = side_by_side((key_local, value_local), CTX, 0, 1)
    row_max, row_sum, weighted = sweep_keys(initial, all_keys, all_values, 0, forward_tile)
    log_norm = row_max + jnp.log(row_sum)
    attention_own = (
        (weighted / row_sum[..., None])
        .transpose(2, 0, 1, 3)
        .reshape(tok_dev, -1)
        .astype(jnp.bfloat16)
    )
    row_delta = jnp.sum(
        grad_grouped.astype(jnp.float32)
        * attention_own.reshape(tok_dev, kv_heads, group_size, HEAD_SIZE).astype(jnp.float32),
        axis=-1,
    ).transpose(1, 2, 0)

    def backward_parts(key_tile, value_tile, allowed):
        scores, key_heads = tile_scores(key_tile)
        masked = jnp.where(allowed, scores, mask_value)
        probability = jnp.where(allowed, jnp.exp(masked - log_norm[..., None]), 0.0)
        value_heads = value_tile.reshape(value_tile.shape[0], kv_heads, HEAD_SIZE)
        dprob = jnp.einsum(
            "tkgd,skd->kgts", grad_grouped, value_heads, preferred_element_type=jnp.float32
        )
        dscore = probability * (dprob - row_delta[..., None])
        return (probability, dscore, key_heads)

    total_keys = all_keys.shape[0]
    query_zero = jnp.zeros((tok_dev, kv_heads, group_size, HEAD_SIZE), jnp.float32)
    joint_rows = 512
    joint_count = total_keys // joint_rows

    def joint_tile(running, inputs):
        tile_index, key_tile, value_tile = inputs
        allowed = tile_mask(query_docs, positions, doc_ids, tile_index * joint_rows, joint_rows)

        def compute(current):
            probability, dscore, key_heads = backward_parts(key_tile, value_tile, allowed)
            dscore_low = dscore.astype(jnp.bfloat16)
            current = current + jnp.einsum(
                "kgts,skd->tkgd", dscore_low, key_heads, preferred_element_type=jnp.float32
            )
            key_grad = (
                jnp.einsum(
                    "kgts,tkgd->skd", dscore_low, grouped, preferred_element_type=jnp.float32
                )
                * score_scale
            )
            value_grad = jnp.einsum(
                "kgts,tkgd->skd",
                probability.astype(jnp.bfloat16),
                grad_grouped,
                preferred_element_type=jnp.float32,
            )
            return (
                current,
                jnp.concatenate(
                    [key_grad.reshape(joint_rows, -1), value_grad.reshape(joint_rows, -1)], axis=1
                ),
            )

        def skipped(current):
            return (current, jnp.zeros((joint_rows, 2 * kv_heads * HEAD_SIZE), jnp.float32))

        return lax.cond(jnp.any(allowed), compute, skipped, running)

    query_sum, stacked = lax.scan(
        joint_tile,
        query_zero,
        (
            jnp.arange(joint_count, dtype=jnp.int32),
            all_keys.reshape(joint_count, joint_rows, -1),
            all_values.reshape(joint_count, joint_rows, -1),
        ),
    )
    kv_grad = scatter_axes(stacked.reshape(total_keys, -1).astype(jnp.bfloat16), CTX, 0).astype(
        jnp.float32
    )
    query_grad_own = (query_sum * score_scale).reshape(tok_dev, -1).astype(jnp.bfloat16)
    key_grad_local = kv_grad[:, : kv_heads * HEAD_SIZE].astype(jnp.bfloat16)
    value_grad_local = kv_grad[:, kv_heads * HEAD_SIZE :].astype(jnp.bfloat16)
    key_gradient, value_gradient = (
        lax.all_to_all(key_grad_local, "head", split_axis=0, concat_axis=1, tiled=True),
        lax.all_to_all(value_grad_local, "head", split_axis=0, concat_axis=1, tiled=True),
    )
    natural = log_norm.reshape(-1, shards, block_rows)[:, send_order, :]
    owned_lse = lax.all_to_all(natural, CTX, split_axis=1, concat_axis=1, tiled=True).reshape(
        -1, tok_dev
    )
    return (attention_own, owned_lse, query_grad_own, key_gradient, value_gradient)


def solution(mesh):
    finer = Mesh(mesh.devices.reshape(8, 4, mesh.shape["head"]), ("ctx_0", "ctx_1", "head"))
    return jax.shard_map(
        body,
        mesh=finer,
        in_specs=(P(CTX, "head"), P(CTX_HEAD, None), P(CTX_HEAD, None), P(CTX, "head"), P(), P()),
        out_specs=(
            P(CTX, "head"),
            P("head", CTX),
            P(CTX, "head"),
            P(CTX_HEAD, None),
            P(CTX_HEAD, None),
        ),
        check_vma=False,
    )
```

profile of v0, /device:TPU:65, one launch (start us, length us, event | category | flops | bytes accessed | tf_op | source)
XLA Modules:
  0.0 275.4 jit_solution(16283803853437525407)
XLA Ops:
  8.6 5.0 %all-to-all-start = ((bf16[16,8,128]{2,0,1:T(8,128)(2,1)}), bf16[16,8,128]{2,0,1:T(8,128)(2,1)S(1)}, u32[]{:S(2)}, u32[]{:S(2)}) async-start(bf16[16,8,128]{2,0,1:T(8,128)(2,1)} %copy_bitcast_fusion.3), calls=%async_computation | async-start | bytes 65536 | tf_op jit(solution)/shard_map/all_to_all | solution.py:65
  14.3 4.0 %all-to-all-done = bf16[16,8,128]{2,0,1:T(8,128)(2,1)S(1)} async-done(((bf16[16,8,128]{2,0,1:T(8,128)(2,1)}), bf16[16,8,128]{2,0,1:T(8,128)(2,1)S(1)}, u32[]{:S(2)}, u32[]{:S(2)}) %all-to-all-start) | async-done | bytes 32800 | tf_op jit(solution)/shard_map/all_to_all | solution.py:65
  18.2 7.8 %all_to_all.81 = bf16[16,8,128]{2,0,1:T(8,128)(2,1)S(1)} all-to-all(bf16[16,8,128]{2,0,1:T(8,128)(2,1)S(1)} %copy_bitcast_fusion.2), channel_id=1, replica_groups=mesh['ctx_0'=8,'ctx_1'=4,'head'=8] {'head'}, dimensions={1} | all-to-all | bytes 65536 | tf_op jit(solution)/shard_map/all_to_all | solution.py:66
  26.8 1.1 copy.94
  28.1 1.1 copy.100
  29.3 1.1 gather_fusion
  30.4 70.0 %all-gather.2.cloned.1.call-done = bf16[4096,256]{1,0:T(8,128)(2,1)} async-done(((bf16[128,256]{1,0:T(8,128)(2,1)}), bf16[4096,256]{1,0:T(8,128)(2,1)}) %all-gather.2.cloned.1.call-update) | async-done | bytes 2097168 | tf_op jit(solution)/shard_map/all_gather | solution.py:17
  100.4 2.7 fusion.54
  103.1 31.3 %while.31 = (s32[]{:T(128)}, f32[1,8,128]{2,1,0:T(8,128)S(1)}, f32[1,8,128]{2,1,0:T(8,128)S(1)}, f32[1,8,128,128]{3,2,1,0:T(8,128)S(1)}, s32[128]{0:T(128)S(1)},...) while((s32[]{:T(128)}, f32[1,8,128]{2,1,0:T(8,128)S(1)}, ...), condition=%wide.region_6.7_spmd.clone, body=%wide.region_0.6_spmd.clone.sunk | while | flops 275779200 | bytes 8204637 | solution.py:46
  105.9 2.8 %conditional.6 = ((f32[1,8,128]{2,1,0:T(8,128)S(1)}, f32[1,8,128]{2,1,0:T(8,128)S(1)}, f32[1,8,128,128]{3,2,1,0:T(8,128)S(1)})) conditional(s32[]{:T(128)} %convert_element_type.94, (f32[1,8,128]{2,1,0:T(8,128)S(1)}, f32[1,8,128]{2,1,0:T(8,128)S(1)}, f32[1,8,128,128]{3,2,1,0:T(8,128)S(1)}) %tuple.90, (pred[128,512]{0,1:T(8,128)(4,1)S(1)}, ...), branch_computations={%region_2.2_spmd, %region_3.5_spmd} | conditional | flops 275516416 | bytes 8127012 | solution.py:106
  106.4 1.7 fusion.7
  111.6 2.8 %conditional.6 = ((f32[1,8,128]{2,1,0:T(8,128)S(1)}, f32[1,8,128]{2,1,0:T(8,128)S(1)}, f32[1,8,128,128]{3,2,1,0:T(8,128)S(1)})) conditional(s32[]{:T(128)} %convert_element_type.94, (f32[1,8,128]{2,1,0:T(8,128)S(1)}, f32[1,8,128]{2,1,0:T(8,128)S(1)}, f32[1,8,128,128]{3,2,1,0:T(8,128)S(1)}) %tuple.90, (pred[128,512]{0,1:T(8,128)(4,1)S(1)}, ...), branch_computations={%region_2.2_spmd, %region_3.5_spmd} | conditional | flops 275516416 | bytes 8127012 | solution.py:106
  112.1 1.7 fusion.7
  117.2 2.8 %conditional.6 = ((f32[1,8,128]{2,1,0:T(8,128)S(1)}, f32[1,8,128]{2,1,0:T(8,128)S(1)}, f32[1,8,128,128]{3,2,1,0:T(8,128)S(1)})) conditional(s32[]{:T(128)} %convert_element_type.94, (f32[1,8,128]{2,1,0:T(8,128)S(1)}, f32[1,8,128]{2,1,0:T(8,128)S(1)}, f32[1,8,128,128]{3,2,1,0:T(8,128)S(1)}) %tuple.90, (pred[128,512]{0,1:T(8,128)(4,1)S(1)}, ...), branch_computations={%region_2.2_spmd, %region_3.5_spmd} | conditional | flops 275516416 | bytes 8127012 | solution.py:106
  117.7 1.7 fusion.7
  134.7 39.9 %while.32 = (s32[]{:T(128)}, f32[128,1,8,128]{0,3,2,1:T(8,128)S(1)}, bf16[8,512,256]{2,1,0:T(8,128)(2,1)}, s32[128]{0:T(128)S(1)}, s32[8]{0:T(128)S(1)}, /*index...) while((s32[]{:T(128)}, ...), condition=%wide.region_13.14_spmd.clone, body=%wide.region_9.13_spmd.clone.sunk | while | flops 676332160 | bytes 13914961 | solution.py:178
  137.6 3.4 %conditional.7 = (f32[128,1,8,128]{0,3,2,1:T(8,128)S(1)}, bf16[1,512,256]{1,2,0:T(8,128)(2,1)S(1)}) conditional(s32[]{:T(128)} %convert_element_type.95, f32[128,1,8,128]{0,3,2,1:T(8,128)S(1)} %get-tuple-element.726, (bf16[8,512,128]{2,1,0:T(8,128)(2,1)S(1)}, s32[]{:T(128)}, pred[128,512]{0,1:T(8,128)(4,1)S(1)}, ...), branch_computations={%region_11.11_spmd, %region_12.12_spmd} | conditional | flops 676069376 | bytes 12788248 | solution.py:176
  138.3 1.3 fusion.32
  144.6 3.4 %conditional.7 = (f32[128,1,8,128]{0,3,2,1:T(8,128)S(1)}, bf16[1,512,256]{1,2,0:T(8,128)(2,1)S(1)}) conditional(s32[]{:T(128)} %convert_element_type.95, f32[128,1,8,128]{0,3,2,1:T(8,128)S(1)} %get-tuple-element.726, (bf16[8,512,128]{2,1,0:T(8,128)(2,1)S(1)}, s32[]{:T(128)}, pred[128,512]{0,1:T(8,128)(4,1)S(1)}, ...), branch_computations={%region_11.11_spmd, %region_12.12_spmd} | conditional | flops 676069376 | bytes 12788248 | solution.py:176
  145.3 1.3 fusion.32
  151.7 3.4 %conditional.7 = (f32[128,1,8,128]{0,3,2,1:T(8,128)S(1)}, bf16[1,512,256]{1,2,0:T(8,128)(2,1)S(1)}) conditional(s32[]{:T(128)} %convert_element_type.95, f32[128,1,8,128]{0,3,2,1:T(8,128)S(1)} %get-tuple-element.726, (bf16[8,512,128]{2,1,0:T(8,128)(2,1)S(1)}, s32[]{:T(128)}, pred[128,512]{0,1:T(8,128)(4,1)S(1)}, ...), branch_computations={%region_11.11_spmd, %region_12.12_spmd} | conditional | flops 676069376 | bytes 12788248 | solution.py:176
  152.4 1.3 fusion.32
  174.7 44.4 %reduce-scatter.3.cloned.1.call-done = bf16[512,256]{1,0:T(8,128)(2,1)} async-done(((bf16[4096,256]{1,0:T(8,128)(2,1)}), bf16[512,256]{1,0:T(8,128)(2,1)}) %reduce-scatter.3.cloned.1.call-update) | async-done | bytes 262160 | tf_op jit(solution)/shard_map/reduce_scatter | solution.py:27
  220.3 1.2 gather_fusion.1
  221.5 7.7 %all-to-all-start.2 = ((f32[8,32,4]{0,2,1:T(4,128)}), f32[8,32,4]{0,2,1:T(4,128)S(1)}, u32[]{:S(2)}, u32[]{:S(2)}) async-start(f32[8,32,4]{0,2,1:T(4,128)} %bitcast.46), calls=%async_computation.2 | async-start | bytes 131072 | tf_op jit(solution)/shard_map/all_to_all | solution.py:198
  229.2 17.2 %reduce-scatter.5.cloned.1.call-done = bf16[128,256]{1,0:T(8,128)(2,1)} async-done(((bf16[512,256]{1,0:T(8,128)(2,1)}), bf16[128,256]{1,0:T(8,128)(2,1)}) %reduce-scatter.5.cloned.1.call-update) | async-done | bytes 65552 | tf_op jit(solution)/shard_map/reduce_scatter | solution.py:27
  246.5 1.4 fusion.55
  247.9 7.0 %all-to-all-start.3 = ((bf16[8,16,128]{2,1,0:T(8,128)(2,1)}), bf16[8,16,128]{2,1,0:T(8,128)(2,1)S(1)}, u32[]{:S(2)}, u32[]{:S(2)}) async-start(bf16[8,16,128]{2,1,0:T(8,128)(2,1)} %bitcast.53), calls=%async_computation.5 | async-start | bytes 65536 | tf_op jit(solution)/shard_map/all_to_all | solution.py:194
  254.9 0.9 copy.114
  257.3 2.3 all-to-all-done.3
  259.6 4.0 %all-to-all-start.4 = ((bf16[8,16,128]{2,1,0:T(8,128)(2,1)}), bf16[8,16,128]{2,1,0:T(8,128)(2,1)S(1)}, u32[]{:S(2)}, u32[]{:S(2)}) async-start(bf16[8,16,128]{2,1,0:T(8,128)(2,1)} %bitcast.55), calls=%async_computation.6 | async-start | bytes 65536 | tf_op jit(solution)/shard_map/all_to_all | solution.py:195
  264.1 4.1 %all-to-all-done.4 = bf16[8,16,128]{2,1,0:T(8,128)(2,1)S(1)} async-done(((bf16[8,16,128]{2,1,0:T(8,128)(2,1)}), bf16[8,16,128]{2,1,0:T(8,128)(2,1)S(1)}, u32[]{:S(2)}, u32[]{:S(2)}) %all-to-all-start.4) | async-done | bytes 32800 | tf_op jit(solution)/shard_map/all_to_all | solution.py:195
  (182 shorter events, 47.7 us)
Async XLA Ops:
  7.2 0.8 copy-start
  7.2 22.1 %copy-start.1 = (s32[4096]{0:T(1024)S(1)}, s32[4096]{0:T(1024)}, u32[]{:S(2)}) copy-start(s32[4096]{0:T(1024)} %param.18) | copy-start | bytes 49156
  8.6 9.7 %all-to-all-start = ((bf16[16,8,128]{2,0,1:T(8,128)(2,1)}), bf16[16,8,128]{2,0,1:T(8,128)(2,1)S(1)}, u32[]{:S(2)}, u32[]{:S(2)}) async-start(bf16[16,8,128]{2,0,1:T(8,128)(2,1)} %copy_bitcast_fusion.3), calls=%async_computation | async-start | bytes 65536 | tf_op jit(solution)/shard_map/all_to_all | solution.py:65
  13.5 86.9 %all-gather.2.cloned.1.call-start = ((), (), s32[]{:S(2)}) async-start(), calls=%async_computation.7 | async-start | bytes 2162688 | tf_op jit(solution)/shard_map/all_gather | solution.py:17
  26.7 192.4 %reduce-scatter.3.cloned.1.call-start = ((), (), s32[]{:S(2)}) async-start(), calls=%async_computation.8 | async-start | bytes 2359296 | tf_op jit(solution)/shard_map/reduce_scatter | solution.py:27
  174.6 44.5 %copy-start.2 = (s32[32,32]{1,0:T(8,128)S(1)}, s32[32,32]{1,0:T(8,128)}, u32[]{:S(2)}) copy-start(s32[32,32]{1,0:T(8,128)} %param.19) | copy-start | bytes 12292
  174.7 71.8 %reduce-scatter.5.cloned.1.call-start = ((), (), s32[]{:S(2)}) async-start(), calls=%async_computation.9 | async-start | bytes 327680 | tf_op jit(solution)/shard_map/reduce_scatter | solution.py:27
  221.5 26.3 %all-to-all-start.2 = ((f32[8,32,4]{0,2,1:T(4,128)}), f32[8,32,4]{0,2,1:T(4,128)S(1)}, u32[]{:S(2)}, u32[]{:S(2)}) async-start(f32[8,32,4]{0,2,1:T(4,128)} %bitcast.46), calls=%async_computation.2 | async-start | bytes 131072 | tf_op jit(solution)/shard_map/all_to_all | solution.py:198
  247.9 11.7 %all-to-all-start.3 = ((bf16[8,16,128]{2,1,0:T(8,128)(2,1)}), bf16[8,16,128]{2,1,0:T(8,128)(2,1)S(1)}, u32[]{:S(2)}, u32[]{:S(2)}) async-start(bf16[8,16,128]{2,1,0:T(8,128)(2,1)} %bitcast.53), calls=%async_computation.5 | async-start | bytes 65536 | tf_op jit(solution)/shard_map/all_to_all | solution.py:194
  259.6 8.7 %all-to-all-start.4 = ((bf16[8,16,128]{2,1,0:T(8,128)(2,1)}), bf16[8,16,128]{2,1,0:T(8,128)(2,1)S(1)}, u32[]{:S(2)}, u32[]{:S(2)}) async-start(bf16[8,16,128]{2,1,0:T(8,128)(2,1)} %bitcast.55), calls=%async_computation.6 | async-start | bytes 65536 | tf_op jit(solution)/shard_map/all_to_all | solution.py:195
Sparse Core Ops, SparseCore 0:
  26.8 73.5 all-gather.1
  174.8 44.2 reduce-scatter.2
  221.6 24.8 reduce-scatter.4
where the time goes:
time: 278 us; the launch traced here: 275 us
  waiting for transfers between devices  142 us (51%)
  local copies, waits for them, and re-layouts  32.8 us (12%)
  starting transfers between devices  23.7 us (9%)
  loops' own time  22 us (8%)
  other arithmetic  16.8 us (6%)
  matrix products  16.4 us (6%)
  between operations  13.9 us (5%)
  blocking collectives  7.8 us (3%)
    all_gather x1, waiting for transfers between devices, side_by_side(): out, at, done = (lax.all_gather(both, axis, axis=dim, tiled=True), 0, [])  70 us
    reduce_scatter x2, waiting for transfers between devices, scatter_axes(): nearer = lax.psum_scatter(value, axes[0], scatter_dimension=dim, tiled=True)  61.6 us
    another operation x1, loops' own time, sweep_keys(): lax.scan(advance, carried, (jnp.arange(tile_count, dtype=jnp.int32), keys...  10.7 us
    another operation x1, loops' own time, body(): lax.scan(joint_tile, query_zero, (jnp.arange(joint_count, dtype=jnp.int32...  10.7 us
    dynamic_slice x16, local copies, waits for them, and re-layouts, sweep_keys(): lax.scan(advance, carried, (jnp.arange(tile_count, dtype=jnp.int32), keys...  9.35 us
    all_to_all x1, blocking collectives, body(): lax.all_to_all(value_matrix_rows, 'head', split_axis=1, concat_axis=0, ti...  7.8 us
    all_to_all x1, starting transfers between devices, body(): lax.all_to_all(natural, CTX, split_axis=1, concat_axis=1, tiled=True)  7.67 us
    all_to_all x1, starting transfers between devices, body(): lax.all_to_all(key_grad_local, 'head', split_axis=0, concat_axis=1, tiled...  6.96 us
  transfers between devices with their start and end apart: 7, of which 6 were waited for; matrix products, arithmetic and copies ran while one was open for 4% of the time, Pallas kernels for 0%

commit v1 on v0

v1 whole, which is shorter than its diff:
```python
import jax
import jax.numpy as jnp
from jax import lax
from jax.experimental import pallas as pl
from jax.experimental.pallas import tpu as pltpu
from jax.sharding import PartitionSpec as P

D = 128
TOK = 128
HG = 8
ROWS = HG * TOK
CHUNK = 256
NCHUNK = ROWS // CHUNK
NZ, NY = 8, 4
NH = 8
TOKDEV = 16
OWN = 16
LOG2E = 1.4426950408889634
LN2 = 0.6931471805599453
NEG = -1e30
SCALE = D**-0.5
F32 = jnp.float32
BF16 = jnp.bfloat16
MESH = pl.DeviceIdType.MESH


def dot(a, b):
    return jnp.dot(a, b, preferred_element_type=F32)


def kernel(
    q_hbm, k_ref, v_ref, g_hbm, doc_ref, owner_ref,
    att_ref, lse_ref, gq_ref, gk_ref, gv_ref,
    q_in, g_in, qt, gt, qs, gs, kv, stage, pbuf, dsb, plb, tr, ot, dqt, mrun, lrun, mgrp, delta,
    part, yrecv, zrecv, zsend, total, hrecv, lown, lgat,
    load_sem, ha_send, ha_recv, kz_send, ky_send, kv_recv,
    gy_send, gy_recv, gz_send, gz_recv, hb_send, hb_recv, ly_send, ly_recv, lz_send, lz_recv,
):
    ctx = lax.axis_index("ctx")
    head = lax.axis_index("head")
    z = ctx // NY
    y = ctx % NY

    load_q = pltpu.make_async_copy(q_hbm, q_in, load_sem.at[0])
    load_g = pltpu.make_async_copy(g_hbm, g_in, load_sem.at[1])
    load_q.start()
    load_g.start()

    def at_head(i):
        return (ctx, (head + i) % NH)

    def at_y(i):
        return (z * NY + (y + i) % NY, head)

    def at_z(i):
        return (((z + i) % NZ) * NY + y, head)

    barrier = pltpu.get_barrier_semaphore()
    for i in range(1, NH):
        pl.semaphore_signal(barrier, inc=1, device_id=at_head(i), device_id_type=MESH)
    for i in range(1, NY):
        pl.semaphore_signal(barrier, inc=1, device_id=at_y(i), device_id_type=MESH)
    for i in range(1, NZ):
        pl.semaphore_signal(barrier, inc=1, device_id=at_z(i), device_id_type=MESH)

    for h in range(NH):
        stage[h, 0] = k_ref[:, h * D : (h + 1) * D]
        stage[h, 1] = v_ref[:, h * D : (h + 1) * D]
    pl.semaphore_wait(barrier, NH + NY + NZ - 3)

    def remote(src, dst, ssem, rsem, to):
        return pltpu.make_async_remote_copy(
            src_ref=src, dst_ref=dst, send_sem=ssem, recv_sem=rsem, device_id=to, device_id_type=MESH
        )

    def head_copy(i):
        to = (head + i) % NH
        rows = pl.ds(pl.multiple_of(head * TOKDEV, TOKDEV), TOKDEV)
        return remote(
            stage.at[to], kv.at[OWN, :, rows, :], ha_send.at[i], ha_recv.at[i], at_head(i)
        )

    def head_arrival(i):
        rows = pl.ds(pl.multiple_of(((head + NH - i) % NH) * TOKDEV, TOKDEV), TOKDEV)
        return remote(stage.at[0], kv.at[OWN, :, rows, :], ha_send.at[i], ha_recv.at[i], at_head(i))

    for i in range(1, NH):
        head_copy(i).start()
    kv[OWN, :, pl.ds(pl.multiple_of(head * TOKDEV, TOKDEV), TOKDEV), :] = stage[head]

    load_q.wait()
    load_g.wait()
    for h in range(HG):
        cols = slice(h * D, (h + 1) * D)
        qh, gh = q_in[:, cols], g_in[:, cols]
        qs[cols, :] = qh
        gs[cols, :] = gh
        qt[:, cols] = qh.T
        gt[:, cols] = gh.T

    @pl.when(z < 4)
    def _():
        for j in range(NY):

            @pl.when(y <= j)
            def _(j=j):
                kv[12 + j] = jnp.zeros((2, TOK, D), BF16)

    for i in range(1, NH):
        head_arrival(i).wait_recv()

    def chain_copy(hop):
        src = kv.at[OWN] if hop == 1 else kv.at[4 * (hop - 2) + y]
        dst = kv.at[4 * (hop - 1) + y]
        to = (jnp.minimum(z + 1, NZ - 1) * NY + y, head)
        return remote(src, dst, kz_send.at[hop - 1], kv_recv.at[4 * (hop - 1) + y], to)

    def chain_goes(hop):
        return (z < NZ - 1) & (z >= hop - 1)

    def chain_start(hop):
        @pl.when(chain_goes(hop))
        def _():
            chain_copy(hop).start()

    def spread_copy(level, i):
        src = kv.at[OWN] if level == 0 else kv.at[4 * (level - 1) + y]
        slot = 12 + y if level in (0, 4) else 4 * (level - 1) + y
        return remote(src, kv.at[slot], ky_send.at[3 * level + i - 1], kv_recv.at[slot], at_y(i))

    def spread_goes(level, i):
        if level == 0:
            return (y + i) < NY
        if level == 4:
            return (z >= 4) & ((y + i) >= NY)
        return z >= level

    def spread_start(level):
        for i in range(1, NY):

            @pl.when(spread_goes(level, i))
            def _(i=i):
                spread_copy(level, i).start()

    def slot_arrival(slot):
        remote(kv.at[slot], kv.at[slot], kz_send.at[0], kv_recv.at[slot], at_y(1)).wait_recv()

    chain_start(1)
    spread_start(0)

    docs = doc_ref[...]
    mine = doc_ref[pl.ds(ctx, 1), :]
    starts = jnp.zeros((1, TOK), F32)
    for v in range(1, 4):
        below = jnp.where(docs < v, 1.0, 0.0).astype(F32)
        count = jnp.sum(jnp.sum(below, axis=0, keepdims=True), axis=1, keepdims=True)
        starts = jnp.where(mine == v, count, starts)
    starts = jnp.concatenate([starts, starts], axis=1)
    tpos = lax.broadcasted_iota(jnp.int32, (1, TOK), 1).astype(F32)
    tpos = jnp.concatenate([tpos, tpos], axis=1) + (ctx * TOK).astype(F32)

    def positions(bases):
        step = lax.broadcasted_iota(jnp.int32, (TOK, 1), 0).astype(F32)
        return jnp.concatenate([step + b.astype(F32) for b in bases], axis=0)

    def chunk_of(c):
        return pl.ds(pl.multiple_of(c * CHUNK, CHUNK), CHUNK)

    def forward(group, slot0, count, bases, diagonal):
        n = count * TOK
        keys = kv[slot0 : slot0 + count, 0].reshape(n, D)
        tr[:, :n] = kv[slot0 : slot0 + count, 1].reshape(n, D).T
        kpos = positions(bases)

        def step(c, carry):
            cols = chunk_of(c)
            s = dot(keys, qt[:, cols]) * (SCALE * LOG2E)
            allowed = kpos >= starts
            if diagonal:
                allowed = allowed & (kpos <= tpos)
            s = jnp.where(allowed, s, NEG)
            top = jnp.max(s, axis=0, keepdims=True)
            if not diagonal:
                before = mrun[:, cols]
                top = jnp.maximum(before, top)
                fade = jnp.exp2(before - top)
            p = jnp.exp2(s - top)
            mass = jnp.sum(p, axis=0, keepdims=True)
            low = p.astype(BF16)
            pbuf[slot0 * TOK : slot0 * TOK + n, cols] = low
            part_o = dot(tr[:, :n], low)
            if diagonal:
                lrun[:, cols] = mass
                ot[:, cols] = part_o
            else:
                lrun[:, cols] = lrun[:, cols] * fade + mass
                ot[:, cols] = ot[:, cols] * fade + part_o
            mrun[:, cols] = top
            mgrp[group : group + 1, cols] = top
            return carry

        lax.fori_loop(0, NCHUNK, step, 0)

    def level_bases(level):
        return [((z - level) * NY + j) * TOK for j in range(NY)]

    mix_bases = [jnp.where(j < y, z * NY + j, (z - 4) * NY + j) * TOK for j in range(NY)]

    def pass_on(level):
        @pl.when(z >= level)
        def _():
            slot_arrival(4 * (level - 1) + y)

        if level < 4:
            chain_start(level + 1)
        spread_start(level)

    def await_level(level):
        @pl.when(z >= level)
        def _():
            for i in range(1, NY):
                slot_arrival(4 * (level - 1) + (y + i) % NY)

    forward(0, OWN, 1, [ctx * TOK], True)
    pass_on(1)
    pass_on(2)
    for level in (1, 2, 3):
        await_level(level)

        @pl.when(z >= level)
        def _(level=level):
            forward(level, 4 * (level - 1), 4, level_bases(level), False)

        if level < 3:
            pass_on(level + 2)
    for i in range(1, NY):
        other = (y + i) % NY

        @pl.when((other < y) | (z >= 4))
        def _(other=other):
            slot_arrival(12 + other)

    forward(4, 12, 4, mix_bases, False)

    def finish(c, carry):
        cols = chunk_of(c)
        mass = lrun[:, cols]
        out = (ot[:, cols] / mass).astype(BF16)
        wide = out.astype(F32)
        ot[:, cols] = wide
        delta[:, cols] = jnp.sum(gt[:, cols].astype(F32) * wide, axis=0, keepdims=True)
        return carry

    lax.fori_loop(0, NCHUNK, finish, 0)
    norm = mrun[...] * LN2 + jnp.log(lrun[...])
    for h in range(HG):
        cols = slice(h * D, (h + 1) * D)
        lown[h : h + 1, :] = norm[:, cols]
    reps = lax.broadcasted_iota(jnp.int32, (32, TOK), 1) // 4 == lax.broadcasted_iota(
        jnp.int32, (32, TOK), 0
    )
    owners = dot(owner_ref[pl.ds(ctx, 1), :].astype(F32), jnp.where(reps, 1.0, 0.0).astype(F32))
    to_col = lax.broadcasted_iota(jnp.int32, (TOK, TOK), 0)
    from_tok = lax.broadcasted_iota(jnp.int32, (TOK, TOK), 1)
    hit = (owners == (to_col // 4).astype(F32)) & (to_col % 4 == from_tok % 4)
    lgat[z, y] = lax.dot_general(
        lown[...],
        jnp.where(hit, 1.0, 0.0).astype(F32),
        (((1,), (1,)), ((), ())),
        precision=lax.Precision.HIGHEST,
        preferred_element_type=F32,
    )

    def lse_y(i):
        return remote(lgat.at[z, y], lgat.at[z, y], ly_send.at[i], ly_recv.at[i], at_y(i))

    def lse_y_arrival(i):
        other = (y + NY - i) % NY
        return remote(lgat.at[z, other], lgat.at[z, other], ly_send.at[i], ly_recv.at[i], at_y(i))

    def lse_z(i):
        return remote(lgat.at[z], lgat.at[z], lz_send.at[i], lz_recv.at[i], at_z(i))

    def lse_z_arrival(i):
        other = (z + NZ - i) % NZ
        return remote(lgat.at[other], lgat.at[other], lz_send.at[i], lz_recv.at[i], at_z(i))

    for i in range(1, NY):
        lse_y(i).start()

    def backward(group, slot0, count, first):
        n = count * TOK
        tr[:, :n] = kv[slot0 : slot0 + count, 0].reshape(n, D).T
        values = kv[slot0 : slot0 + count, 1].reshape(n, D)

        def step(c, carry):
            cols = chunk_of(c)
            share = jnp.exp2(mgrp[group : group + 1, cols] - mrun[:, cols]) / lrun[:, cols]
            p = pbuf[slot0 * TOK : slot0 * TOK + n, cols].astype(F32) * share
            dp = dot(values, gt[:, cols])
            ds = (p * (dp - delta[:, cols])).astype(BF16)
            plb[:n, cols] = p.astype(BF16)
            dsb[:n, cols] = ds
            dq = dot(tr[:, :n], ds)
            if first:
                dqt[:, cols] = dq
            else:
                dqt[:, cols] += dq
            return carry

        lax.fori_loop(0, NCHUNK, step, 0)
        part[slot0 : slot0 + count, 0] = dot(dsb[:n, :], qs[...]).astype(BF16).reshape(count, TOK, D)
        part[slot0 : slot0 + count, 1] = dot(plb[:n, :], gs[...]).astype(BF16).reshape(count, TOK, D)

    def grad_y(g, i):
        other = (y + i) % NY
        return remote(
            part.at[4 * g + other], yrecv.at[g, y], gy_send.at[3 * g + i - 1],
            gy_recv.at[4 * g + y], at_y(i),
        )

    def grad_y_goes(g, i):
        return ((y + i) >= NY) | (z >= 4) if g == 3 else z >= g + 1

    def grad_y_start(g):
        for i in range(1, NY):

            @pl.when(grad_y_goes(g, i))
            def _(i=i):
                grad_y(g, i).start()

    def grad_y_arrival(g, other):
        remote(
            yrecv.at[g, other], yrecv.at[g, other], gy_send.at[0], gy_recv.at[4 * g + other], at_y(1)
        ).wait_recv()

    def grad_z(level):
        to = (jnp.maximum(z - 1, 0) * NY + y, head)
        return remote(
            zsend.at[level - 1], zrecv.at[level - 1], gz_send.at[level - 1], gz_recv.at[level - 1], to
        )

    def wide(ref, *at):
        return ref[at].astype(F32)

    def reduce_level(level):
        g = level - 1

        @pl.when(z >= level)
        def _():
            total[...] = wide(part, 4 * g + y)
            for i in range(1, NY):
                other = (y + i) % NY
                if level == 4:

                    @pl.when(other < y)
                    def _(other=other):
                        grad_y_arrival(g, other)
                        total[...] += wide(yrecv, g, other)
                else:
                    grad_y_arrival(g, other)
                    total[...] += wide(yrecv, g, other)
            if level < 4:

                @pl.when(z < NZ - 1)
                def _():
                    grad_z(level + 1).wait_recv()
                    total[...] += wide(zrecv, level)

            zsend[level - 1] = total[...].astype(BF16)
            grad_z(level).start()

    backward(4, 12, 4, True)
    grad_y_start(3)
    for i in range(1, NY):
        lse_y_arrival(i).wait_recv()
    for i in range(1, NZ):
        lse_z(i).start()
    for level in (3, 2, 1):

        @pl.when(z >= level)
        def _(level=level):
            backward(level, 4 * (level - 1), 4, False)

        grad_y_start(level - 1)
        reduce_level(level + 1)
    backward(0, OWN, 1, False)
    reduce_level(1)
    total[...] = wide(part, OWN)
    for i in range(1, NY):
        other = (y + i) % NY

        @pl.when(other > y)
        def _(other=other):
            grad_y_arrival(3, other)
            total[...] += wide(yrecv, 3, other)

    for h in range(HG):
        cols = slice(h * D, (h + 1) * D)
        att_ref[:, cols] = ot[:, cols].T.astype(BF16)
        gq_ref[:, cols] = (dqt[:, cols] * SCALE).T.astype(BF16)

    for i in range(1, NZ):
        lse_z_arrival(i).wait_recv()
    lane = lax.broadcasted_iota(jnp.int32, (HG, TOK), 1) // 4
    owned = jnp.zeros((HG, TOK), F32)
    for d in range(NZ * NY):
        moved = pltpu.roll(lgat[d // NY, d % NY], ((d - ctx) * 4) % TOK, 1)
        owned = jnp.where(lane == d, moved, owned)
    lse_ref[...] = owned

    @pl.when(z < NZ - 1)
    def _():
        grad_z(1).wait_recv()
        total[...] += wide(zrecv, 0)

    part[OWN, 0] = (total[0] * SCALE).astype(BF16)
    part[OWN, 1] = total[1].astype(BF16)

    def home(i):
        rows = pl.ds(pl.multiple_of(((head + i) % NH) * TOKDEV, TOKDEV), TOKDEV)
        return remote(
            part.at[OWN, :, rows, :], hrecv.at[head], hb_send.at[i], hb_recv.at[i], at_head(i)
        )

    def home_arrival(i):
        other = (head + NH - i) % NH
        return remote(hrecv.at[other], hrecv.at[other], hb_send.at[i], hb_recv.at[i], at_head(i))

    for i in range(1, NH):
        home(i).start()
    hrecv[head] = part[OWN, :, pl.ds(pl.multiple_of(head * TOKDEV, TOKDEV), TOKDEV), :]

    for i in range(1, NH):
        head_copy(i).wait_send()
    for hop in range(1, 5):

        @pl.when(chain_goes(hop))
        def _(hop=hop):
            chain_copy(hop).wait_send()

        @pl.when(z >= hop)
        def _(hop=hop):
            grad_z(hop).wait_send()

    for level in range(5):
        for i in range(1, NY):

            @pl.when(spread_goes(level, i))
            def _(level=level, i=i):
                spread_copy(level, i).wait_send()

    for g in range(4):
        for i in range(1, NY):

            @pl.when(grad_y_goes(g, i))
            def _(g=g, i=i):
                grad_y(g, i).wait_send()

    for i in range(1, NY):
        lse_y(i).wait_send()
    for i in range(1, NZ):
        lse_z(i).wait_send()
    for i in range(1, NH):
        home_arrival(i).wait_recv()
    for h in range(NH):
        gk_ref[:, h * D : (h + 1) * D] = hrecv[h, 0]
        gv_ref[:, h * D : (h + 1) * D] = hrecv[h, 1]
    for i in range(1, NH):
        home(i).wait_send()


def body(queries, key_rows, value_rows, grad_out, doc_ids, block_owner):
    vmem = pl.BlockSpec(memory_space=pltpu.VMEM)
    anywhere = pl.BlockSpec(memory_space=pl.ANY)
    dma = pltpu.SemaphoreType.DMA
    keys = 17 * TOK
    return pl.pallas_call(
        kernel,
        out_shape=(
            jax.ShapeDtypeStruct((TOK, ROWS), BF16),
            jax.ShapeDtypeStruct((HG, TOK), F32),
            jax.ShapeDtypeStruct((TOK, ROWS), BF16),
            jax.ShapeDtypeStruct((TOKDEV, NH * D), BF16),
            jax.ShapeDtypeStruct((TOKDEV, NH * D), BF16),
        ),
        in_specs=[anywhere, vmem, vmem, anywhere, vmem, vmem],
        out_specs=(vmem,) * 5,
        scratch_shapes=[
            pltpu.VMEM((TOK, ROWS), BF16),
            pltpu.VMEM((TOK, ROWS), BF16),
            pltpu.VMEM((D, ROWS), BF16),
            pltpu.VMEM((D, ROWS), BF16),
            pltpu.VMEM((ROWS, D), BF16),
            pltpu.VMEM((ROWS, D), BF16),
            pltpu.VMEM((17, 2, TOK, D), BF16),
            pltpu.VMEM((NH, 2, TOKDEV, D), BF16),
            pltpu.VMEM((keys, ROWS), BF16),
            pltpu.VMEM((4 * TOK, ROWS), BF16),
            pltpu.VMEM((4 * TOK, ROWS), BF16),
            pltpu.VMEM((D, 4 * TOK), BF16),
            pltpu.VMEM((D, ROWS), F32),
            pltpu.VMEM((D, ROWS), F32),
            pltpu.VMEM((1, ROWS), F32),
            pltpu.VMEM((1, ROWS), F32),
            pltpu.VMEM((8, ROWS), F32),
            pltpu.VMEM((1, ROWS), F32),
            pltpu.VMEM((17, 2, TOK, D), BF16),
            pltpu.VMEM((4, NY, 2, TOK, D), BF16),
            pltpu.VMEM((4, 2, TOK, D), BF16),
            pltpu.VMEM((4, 2, TOK, D), BF16),
            pltpu.VMEM((2, TOK, D), F32),
            pltpu.VMEM((NH, 2, TOKDEV, D), BF16),
            pltpu.VMEM((HG, TOK), F32),
            pltpu.VMEM((NZ, NY, HG, TOK), F32),
            dma((2,)),
            dma((NH,)), dma((NH,)),
            dma((4,)), dma((15,)), dma((17,)),
            dma((12,)), dma((16,)), dma((4,)), dma((4,)),
            dma((NH,)), dma((NH,)),
            dma((NY,)), dma((NY,)), dma((NZ,)), dma((NZ,)),
        ],
        compiler_params=pltpu.CompilerParams(
            collective_id=0, has_side_effects=True, vmem_limit_bytes=48 * 1024 * 1024
        ),
        name="packed_attention",
    )(queries, key_rows, value_rows, grad_out, doc_ids.reshape(32, TOK), block_owner)


def solution(mesh):
    return jax.shard_map(
        body,
        mesh=mesh,
        in_specs=(
            P("ctx", "head"), P(("ctx", "head"), None), P(("ctx", "head"), None),
            P("ctx", "head"), P(), P(),
        ),
        out_specs=(
            P("ctx", "head"), P("head", "ctx"), P("ctx", "head"),
            P(("ctx", "head"), None), P(("ctx", "head"), None),
        ),
        check_vma=False,
    )
```

time: 278 us -> 69.9 us (0.25)
  waiting for transfers between devices: 142 us -> 0 us
  Pallas kernels: 0 us -> 60.8 us
  local copies, waits for them, and re-layouts: 32.8 us -> 8.07 us
  starting transfers between devices: 23.7 us -> 0 us
  loops' own time: 22 us -> 0 us
  other arithmetic: 16.8 us -> 0 us
  matrix products: 16.4 us -> 0 us
  between operations: 13.9 us -> 0.66 us
  blocking collectives: 7.8 us -> 0 us
    all_gather x1 -> x0, waiting for transfers between devices: 70 us -> none  [side_by_side(): out, at, done = (lax.all_gather(both, axis, axis=dim, tiled=True), 0, [])]
    reduce_scatter x2 -> x0, waiting for transfers between devices: 61.6 us -> none  [scatter_axes(): nearer = lax.psum_scatter(value, axes[0], scatter_dimension=dim, tiled=True)]
    pallas_call x0 -> x1, Pallas kernels: none -> 60.8 us  [body(): pl.pallas_call(kernel, out_shape=(jax.ShapeDtypeStruct((TOK, ROWS), BF16)...]
    all_to_all x4 -> x0, starting transfers between devices: 23.6 us -> none  [the longest x1 7.67 us: body(): lax.all_to_all(natural, CTX, split_axis=1, concat_axis=1, tiled=True)]
    another operation x18 -> x0, loops' own time: 22 us -> none  [the longest x1 10.7 us: sweep_keys(): lax.scan(advance, carried, (jnp.arange(tile_count, dtype=jnp.int32), keys...]
    dot_general x21 -> x0, matrix products: 16.4 us -> none  [the longest x3 5.23 us: update(): jnp.einsum('kgts,skd->kgtd', weights_raw.astype(jnp.bfloat16), value_head...]
    reduce_or x16 -> x0, other arithmetic: 13.4 us -> none  [the longest x8 6.7 us: forward_tile(): return lax.cond(jnp.any(allowed), update, lambda running: running, carried)]
    dynamic_slice x33 -> x0, local copies, waits for them, and re-layouts: 10.8 us -> none  [the longest x16 9.35 us: sweep_keys(): lax.scan(advance, carried, (jnp.arange(tile_count, dtype=jnp.int32), keys...]
  transfers between devices with their start and end apart: 7 -> 0, of which waited for: 6 -> 0; matrix products, arithmetic and copies ran while one was open for 4% -> 0% of each run, Pallas kernels for 0% -> 0%
where the time goes in v1:
time: 69.9 us; the launch traced here: 69.6 us
  Pallas kernels  60.8 us (87%)
  local copies, waits for them, and re-layouts  8.07 us (12%)
    pallas_call x1, Pallas kernels, body(): pl.pallas_call(kernel, out_shape=(jax.ShapeDtypeStruct((TOK, ROWS), BF16)...  60.8 us
    unnamed x17, local copies, waits for them, and re-layouts  8.07 us

profile of v1, /device:TPU:65, one launch (start us, length us, event | category | flops | bytes accessed | tf_op | source)
XLA Modules:
  0.0 69.6 jit_solution(12191145618202100176)
XLA Ops:
  0.6 0.0 copy-start
  0.6 0.9 %copy-done = bf16[128,1024]{1,0:T(8,128)(2,1)S(1)} copy-done((bf16[128,1024]{1,0:T(8,128)(2,1)S(1)}, bf16[128,1024]{1,0:T(8,128)(2,1)}, u32[]{:S(2)}) %copy-start) | copy-done | bytes 262168
  1.6 0.0 copy-start.1
  1.6 0.9 %copy-done.1 = bf16[128,1024]{1,0:T(8,128)(2,1)S(1)} copy-done((bf16[128,1024]{1,0:T(8,128)(2,1)S(1)}, bf16[128,1024]{1,0:T(8,128)(2,1)}, u32[]{:S(2)}) %copy-start.1) | copy-done | bytes 262168
  2.5 0.0 copy-start.2
  2.5 0.8 %copy-done.2 = bf16[16,1024]{1,0:T(8,128)(2,1)S(1)} copy-done((bf16[16,1024]{1,0:T(8,128)(2,1)S(1)}, bf16[16,1024]{1,0:T(8,128)(2,1)}, u32[]{:S(2)}) %copy-start.2) | copy-done | bytes 32792
  3.3 0.0 copy-start.3
  3.3 0.8 %copy-done.3 = bf16[16,1024]{1,0:T(8,128)(2,1)S(1)} copy-done((bf16[16,1024]{1,0:T(8,128)(2,1)S(1)}, bf16[16,1024]{1,0:T(8,128)(2,1)}, u32[]{:S(2)}) %copy-start.3) | copy-done | bytes 32792
  4.1 0.0 copy-start.4
  4.1 0.7 %copy-done.4 = s32[4096]{0:T(1024)S(1)} copy-done((s32[4096]{0:T(1024)S(1)}, s32[4096]{0:T(1024)}, u32[]{:S(2)}) %copy-start.4) | copy-done | bytes 16408
  4.8 0.0 copy-start.5
  4.8 0.7 %copy-done.5 = s32[32,32]{1,0:T(8,128)S(1)} copy-done((s32[32,32]{1,0:T(8,128)S(1)}, s32[32,32]{1,0:T(8,128)}, u32[]{:S(2)}) %copy-start.5) | copy-done | bytes 4120
  5.5 60.8 %packed_attention.1 = (bf16[128,1024]{1,0:T(8,128)(2,1)S(1)}, f32[8,128]{1,0:T(8,128)S(1)}, bf16[128,1024]{1,0:T(8,128)(2,1)S(1)}, bf16[16,1024]{1,0:T(8,128)(2,1)S(1)}, bf16[16,1024]{1,0:T(8,128)(2,1)S(1)}) custom-call(bf16[128,1024]{1,0:T(8,128)(2,1)S(1)} %copy-done, bf16[16,1024]{1,0:T(8,128)(2,1)S(1)} %copy-done.2, bf16[16,1024]{1,0:T(8,128)(2,1)S(1)} %copy-done.3, ...), custom_call_target="tpu_custom_call" | custom-call | tf_op jit(solution)/shard_map/packed_attention/pallas_call | solution.py:478
  66.3 0.7 %copy.16 = bf16[128,1024]{1,0:T(8,128)(2,1)} copy(bf16[128,1024]{1,0:T(8,128)(2,1)S(1)} %get-tuple-element.10) | data formatting | bytes 524288
  67.0 0.6 copy.17
  67.6 0.7 %copy.18 = bf16[128,1024]{1,0:T(8,128)(2,1)} copy(bf16[128,1024]{1,0:T(8,128)(2,1)S(1)} %get-tuple-element.12) | data formatting | bytes 524288
  68.3 0.6 copy.19
  68.9 0.6 copy.20
Async XLA Ops:
  0.6 1.0 %copy-start = (bf16[128,1024]{1,0:T(8,128)(2,1)S(1)}, bf16[128,1024]{1,0:T(8,128)(2,1)}, u32[]{:S(2)}) copy-start(bf16[128,1024]{1,0:T(8,128)(2,1)} %q_hbm.1) | copy-start | bytes 786436
  1.6 0.9 %copy-start.1 = (bf16[128,1024]{1,0:T(8,128)(2,1)S(1)}, bf16[128,1024]{1,0:T(8,128)(2,1)}, u32[]{:S(2)}) copy-start(bf16[128,1024]{1,0:T(8,128)(2,1)} %g_hbm.1) | copy-start | bytes 786436
  2.5 0.8 %copy-start.2 = (bf16[16,1024]{1,0:T(8,128)(2,1)S(1)}, bf16[16,1024]{1,0:T(8,128)(2,1)}, u32[]{:S(2)}) copy-start(bf16[16,1024]{1,0:T(8,128)(2,1)} %k_ref.1) | copy-start | bytes 98308
  3.3 0.8 %copy-start.3 = (bf16[16,1024]{1,0:T(8,128)(2,1)S(1)}, bf16[16,1024]{1,0:T(8,128)(2,1)}, u32[]{:S(2)}) copy-start(bf16[16,1024]{1,0:T(8,128)(2,1)} %v_ref.1) | copy-start | bytes 98308
  4.1 0.7 %copy-start.4 = (s32[4096]{0:T(1024)S(1)}, s32[4096]{0:T(1024)}, u32[]{:S(2)}) copy-start(s32[4096]{0:T(1024)} %param.10) | copy-start | bytes 49156
  4.8 0.7 %copy-start.5 = (s32[32,32]{1,0:T(8,128)S(1)}, s32[32,32]{1,0:T(8,128)}, u32[]{:S(2)}) copy-start(s32[32,32]{1,0:T(8,128)} %owner_ref.1) | copy-start | bytes 12292

commit v2 on v1

v2 whole, which is shorter than its diff:
```python
import functools

import jax
import jax.numpy as jnp
from jax import lax
from jax.experimental import pallas as pl
from jax.experimental.pallas import tpu as pltpu
from jax.sharding import PartitionSpec as P

D = 128
TOK = 128
HG = 8
ROWS = HG * TOK
CHUNK = 256
NCHUNK = ROWS // CHUNK
NZ, NY = 8, 4
NH = 8
TOKDEV = 16
OWN = 16
LOG2E = 1.4426950408889634
LN2 = 0.6931471805599453
NEG = -1e30
SCALE = D**-0.5
F32 = jnp.float32
BF16 = jnp.bfloat16
MESH = pl.DeviceIdType.MESH


def dot(a, b):
    return jnp.dot(a, b, preferred_element_type=F32)


def kernel(
    q_hbm, k_hbm, v_hbm, g_hbm, doc_hbm, owner_hbm,
    att_ref, lse_ref, gq_ref, gk_ref, gv_ref,
    q_in, g_in, k_ref, v_ref, doc_ref, owner_ref,
    qt, gt, qs, gs, kv, stage, pbuf, dpb, dsb, kt, tr, ot, dqt, mrun, lrun, mgrp, delta,
    part, yrecv, zrecv, zsend, total, pieces, hrecv, lown, lgat,
    load_sem, ha_send, ha_recv, kz_send, ky_send, kv_recv,
    gy_send, gy_recv, gz_send, gz_recv, hb_send, hb_recv, ly_send, ly_recv, lz_send, lz_recv,
):
    ctx = lax.axis_index("ctx")
    head = lax.axis_index("head")
    z = ctx // NY
    y = ctx % NY

    loads = [
        pltpu.make_async_copy(src, dst, load_sem.at[i])
        for i, (src, dst) in enumerate(
            (
                (k_hbm, k_ref), (v_hbm, v_ref), (q_hbm, q_in), (g_hbm, g_in),
                (doc_hbm, doc_ref), (owner_hbm, owner_ref),
            )
        )
    ]
    for load in loads:
        load.start()

    def at_head(i):
        return (ctx, (head + i) % NH)

    def at_y(i):
        return (z * NY + (y + i) % NY, head)

    def at_z(i):
        return (((z + i) % NZ) * NY + y, head)

    barrier = pltpu.get_barrier_semaphore()
    for i in range(1, NH):
        pl.semaphore_signal(barrier, inc=1, device_id=at_head(i), device_id_type=MESH)
    for i in range(1, NY):
        pl.semaphore_signal(barrier, inc=1, device_id=at_y(i), device_id_type=MESH)
    for i in (1, NZ - 1):
        pl.semaphore_signal(barrier, inc=1, device_id=at_z(i), device_id_type=MESH)

    loads[0].wait()
    loads[1].wait()
    for h in range(NH):
        stage[h, 0] = k_ref[:, h * D : (h + 1) * D]
        stage[h, 1] = v_ref[:, h * D : (h + 1) * D]
    pl.semaphore_wait(barrier, NH + NY)

    def remote(src, dst, ssem, rsem, to):
        return pltpu.make_async_remote_copy(
            src_ref=src, dst_ref=dst, send_sem=ssem, recv_sem=rsem, device_id=to, device_id_type=MESH
        )

    def head_copy(i):
        to = (head + i) % NH
        rows = pl.ds(pl.multiple_of(head * TOKDEV, TOKDEV), TOKDEV)
        return remote(
            stage.at[to], kv.at[OWN, :, rows, :], ha_send.at[i], ha_recv.at[i], at_head(i)
        )

    def head_arrival(i):
        rows = pl.ds(pl.multiple_of(((head + NH - i) % NH) * TOKDEV, TOKDEV), TOKDEV)
        return remote(stage.at[0], kv.at[OWN, :, rows, :], ha_send.at[i], ha_recv.at[i], at_head(i))

    for i in range(1, NH):
        head_copy(i).start()
    kv[OWN, :, pl.ds(pl.multiple_of(head * TOKDEV, TOKDEV), TOKDEV), :] = stage[head]

    for load in loads[2:]:
        load.wait()
    for h in range(HG):
        cols = slice(h * D, (h + 1) * D)
        qh, gh = q_in[:, cols], g_in[:, cols]
        qs[cols, :] = qh
        gs[cols, :] = gh
        qt[:, cols] = qh.T
        gt[:, cols] = gh.T

    @pl.when(z < 4)
    def _():
        for j in range(NY):

            @pl.when(y <= j)
            def _(j=j):
                kv[12 + j] = jnp.zeros((2, TOK, D), BF16)

    for i in range(1, NH):
        head_arrival(i).wait_recv()

    def chain_copy(hop):
        src = kv.at[OWN] if hop == 1 else kv.at[4 * (hop - 2) + y]
        dst = kv.at[4 * (hop - 1) + y]
        to = (jnp.minimum(z + 1, NZ - 1) * NY + y, head)
        return remote(src, dst, kz_send.at[hop - 1], kv_recv.at[4 * (hop - 1) + y], to)

    def chain_goes(hop):
        return (z < NZ - 1) & (z >= hop - 1)

    def chain_start(hop):
        @pl.when(chain_goes(hop))
        def _():
            chain_copy(hop).start()

    def spread_copy(level, i):
        src = kv.at[OWN] if level == 0 else kv.at[4 * (level - 1) + y]
        slot = 12 + y if level in (0, 4) else 4 * (level - 1) + y
        return remote(src, kv.at[slot], ky_send.at[3 * level + i - 1], kv_recv.at[slot], at_y(i))

    def spread_goes(level, i):
        if level == 0:
            return (y + i) < NY
        if level == 4:
            return (z >= 4) & ((y + i) >= NY)
        return z >= level

    def spread_start(level):
        for i in range(1, NY):

            @pl.when(spread_goes(level, i))
            def _(i=i):
                spread_copy(level, i).start()

    def slot_arrival(slot):
        remote(kv.at[slot], kv.at[slot], kz_send.at[0], kv_recv.at[slot], at_y(1)).wait_recv()

    chain_start(1)
    spread_start(0)

    docs = doc_ref[...]
    mine = doc_ref[pl.ds(ctx, 1), :]
    starts = jnp.zeros((1, TOK), F32)
    for v in range(1, 4):
        below = jnp.where(docs < v, 1.0, 0.0).astype(F32)
        count = jnp.sum(jnp.sum(below, axis=0, keepdims=True), axis=1, keepdims=True)
        starts = jnp.where(mine == v, count, starts)
    starts = jnp.concatenate([starts, starts], axis=1)
    tpos = lax.broadcasted_iota(jnp.int32, (1, TOK), 1).astype(F32)
    tpos = jnp.concatenate([tpos, tpos], axis=1) + (ctx * TOK).astype(F32)

    def positions(bases):
        step = lax.broadcasted_iota(jnp.int32, (TOK, 1), 0).astype(F32)
        return jnp.concatenate([step + b.astype(F32) for b in bases], axis=0)

    def chunk_of(c):
        return slice(c * CHUNK, (c + 1) * CHUNK)

    def forward(group, slot0, count, bases, diagonal, halfway=None):
        n = count * TOK
        span = slice(slot0 * TOK, slot0 * TOK + n)
        keys = kv[slot0 : slot0 + count, 0].reshape(n, D)
        values = kv[slot0 : slot0 + count, 1].reshape(n, D)
        kt[:, span] = keys.T
        tr[:, :n] = values.T
        kpos = positions(bases)

        def step(c):
            cols = chunk_of(c)
            s = dot(keys, qt[:, cols]) * (SCALE * LOG2E)
            allowed = kpos >= starts
            if diagonal:
                allowed = allowed & (kpos <= tpos)
            s = jnp.where(allowed, s, NEG)
            top = jnp.max(s, axis=0, keepdims=True)
            if not diagonal:
                before = mrun[:, cols]
                top = jnp.maximum(before, top)
                fade = jnp.exp2(before - top)
            p = jnp.exp2(s - top)
            mass = jnp.sum(p, axis=0, keepdims=True)
            low = p.astype(BF16)
            pbuf[span, cols] = low
            part_o = dot(tr[:, :n], low)
            dpb[span, cols] = dot(values, gt[:, cols])
            if diagonal:
                lrun[:, cols] = mass
                ot[:, cols] = part_o
            else:
                lrun[:, cols] = lrun[:, cols] * fade + mass
                ot[:, cols] = ot[:, cols] * fade + part_o
            mrun[:, cols] = top
            mgrp[group : group + 1, cols] = top
            if halfway is not None and c == NCHUNK // 2 - 1:
                halfway()

        for c in range(NCHUNK):
            step(c)

    def level_bases(level):
        return [((z - level) * NY + j) * TOK for j in range(NY)]

    mix_bases = [jnp.where(j < y, z * NY + j, (z - 4) * NY + j) * TOK for j in range(NY)]

    def pass_on(level):
        @pl.when(z >= level)
        def _():
            slot_arrival(4 * (level - 1) + y)

        if level < 4:
            chain_start(level + 1)
        spread_start(level)

    def await_level(level):
        @pl.when(z >= level)
        def _():
            for i in range(1, NY):
                slot_arrival(4 * (level - 1) + (y + i) % NY)

    forward(0, OWN, 1, [ctx * TOK], True)
    pass_on(1)
    pass_on(2)
    for level in (1, 2, 3):
        await_level(level)
        if level < 3:
            halfway = functools.partial(pass_on, level + 2)

            @pl.when(z < level)
            def _(halfway=halfway):
                halfway()

        else:
            halfway = None

        @pl.when(z >= level)
        def _(level=level, halfway=halfway):
            forward(level, 4 * (level - 1), 4, level_bases(level), False, halfway)

    for i in range(1, NY):
        other = (y + i) % NY

        @pl.when((other < y) | (z >= 4))
        def _(other=other):
            slot_arrival(12 + other)

    forward(4, 12, 4, mix_bases, False)

    def finish(c):
        cols = chunk_of(c)
        mass = lrun[:, cols]
        out = (ot[:, cols] / mass).astype(BF16)
        wide = out.astype(F32)
        ot[:, cols] = wide
        delta[:, cols] = jnp.sum(gt[:, cols].astype(F32) * wide, axis=0, keepdims=True)

    for c in range(NCHUNK):
        finish(c)
    norm = mrun[...] * LN2 + jnp.log(lrun[...])
    for h in range(HG):
        cols = slice(h * D, (h + 1) * D)
        lown[h : h + 1, :] = norm[:, cols]
    reps = lax.broadcasted_iota(jnp.int32, (32, TOK), 1) // 4 == lax.broadcasted_iota(
        jnp.int32, (32, TOK), 0
    )
    owners = dot(owner_ref[pl.ds(ctx, 1), :].astype(F32), jnp.where(reps, 1.0, 0.0).astype(F32))
    to_col = lax.broadcasted_iota(jnp.int32, (TOK, TOK), 0)
    from_tok = lax.broadcasted_iota(jnp.int32, (TOK, TOK), 1)
    hit = (owners == (to_col // 4).astype(F32)) & (to_col % 4 == from_tok % 4)
    lgat[z, y] = lax.dot_general(
        lown[...],
        jnp.where(hit, 1.0, 0.0).astype(F32),
        (((1,), (1,)), ((), ())),
        precision=lax.Precision.HIGHEST,
        preferred_element_type=F32,
    )

    def lse_y(i):
        return remote(lgat.at[z, y], lgat.at[z, y], ly_send.at[i], ly_recv.at[i], at_y(i))

    def lse_y_arrival(i):
        other = (y + NY - i) % NY
        return remote(lgat.at[z, other], lgat.at[z, other], ly_send.at[i], ly_recv.at[i], at_y(i))

    def lse_up(step):
        block = lgat.at[(z + NZ - step) % NZ]
        return remote(block, block, lz_send.at[step], lz_recv.at[step], at_z(1))

    def lse_up_arrival(step):
        block = lgat.at[(z + NZ - 1 - step) % NZ]
        return remote(block, block, lz_send.at[step], lz_recv.at[step], at_z(1))

    def lse_down(step):
        block = lgat.at[(z + step) % NZ]
        return remote(block, block, lz_send.at[4 + step], lz_recv.at[4 + step], at_z(NZ - 1))

    def lse_down_arrival(step):
        block = lgat.at[(z + 1 + step) % NZ]
        return remote(block, block, lz_send.at[4 + step], lz_recv.at[4 + step], at_z(NZ - 1))

    def lse_step(step):
        if step == 0:
            for i in range(1, NY):
                lse_y_arrival(i).wait_recv()
        else:
            lse_up_arrival(step - 1).wait_recv()
            if step < 4:
                lse_down_arrival(step - 1).wait_recv()
        if step < 4:
            lse_up(step).start()
        if step < 3:
            lse_down(step).start()

    for i in range(1, NY):
        lse_y(i).start()

    def backward(group, slot0, count):
        n = count * TOK
        span = slice(slot0 * TOK, slot0 * TOK + n)

        def step(c):
            cols = chunk_of(c)
            share = jnp.exp2(mgrp[group : group + 1, cols] - mrun[:, cols]) / lrun[:, cols]
            p = pbuf[span, cols].astype(F32) * share
            dsb[span, cols] = (p * (dpb[span, cols] - delta[:, cols])).astype(BF16)
            pbuf[span, cols] = p.astype(BF16)

        for c in range(NCHUNK):
            step(c)
        part[slot0 : slot0 + count, 0] = dot(dsb[span, :], qs[...]).astype(BF16).reshape(count, TOK, D)
        part[slot0 : slot0 + count, 1] = dot(pbuf[span, :], gs[...]).astype(BF16).reshape(count, TOK, D)

    def query_gradient(slot0, count, first):
        span = slice(slot0 * TOK, (slot0 + count) * TOK)

        def step(c):
            cols = chunk_of(c)
            dq = dot(kt[:, span], dsb[span, cols])
            if first:
                dqt[:, cols] = dq
            else:
                dqt[:, cols] += dq

        for c in range(NCHUNK):
            step(c)

    def grad_y(g, i):
        other = (y + i) % NY
        return remote(
            part.at[4 * g + other], yrecv.at[g, y], gy_send.at[3 * g + i - 1],
            gy_recv.at[4 * g + y], at_y(i),
        )

    def grad_y_goes(g, i, part_of=None):
        if g < 3:
            return z >= g + 1
        own_level, far_level = (y + i) >= NY, ((y + i) < NY) & (z >= 4)
        return {None: own_level | far_level, 0: own_level, 4: far_level}[part_of]

    def grad_y_start(g, part_of=None):
        for i in range(1, NY):

            @pl.when(grad_y_goes(g, i, part_of))
            def _(i=i):
                grad_y(g, i).start()

    def grad_y_arrival(g, other):
        remote(
            yrecv.at[g, other], yrecv.at[g, other], gy_send.at[0], gy_recv.at[4 * g + other], at_y(1)
        ).wait_recv()

    def wide(ref, *at):
        return ref[at].astype(F32)

    def grad_z(level):
        to = (jnp.maximum(z - (1 if level == 3 else 2), 0) * NY + y, head)
        at = level - 2
        return remote(zsend.at[at], zrecv.at[at], gz_send.at[at], gz_recv.at[at], to)

    def column_sum(level):
        g = level - 1
        total[...] = wide(part, 4 * g + y)
        for i in range(1, NY):
            other = (y + i) % NY
            if level == 4:

                @pl.when(other < y)
                def _(other=other):
                    grad_y_arrival(g, other)
                    total[...] += wide(yrecv, g, other)
            else:
                grad_y_arrival(g, other)
                total[...] += wide(yrecv, g, other)

    def from_z(level):
        grad_z(level).wait_recv()
        total[...] += wide(zrecv, level - 2)

    def reduce_level(level):
        @pl.when(z >= level)
        def _():
            column_sum(level)
            if level == 2:
                pl.when(z < NZ - 2)(lambda: from_z(4))
                pl.when(z < NZ - 1)(lambda: from_z(3))
            zsend[level - 2] = total[...].astype(BF16)
            grad_z(level).start()

    def home_rows(to):
        return pl.ds(pl.multiple_of(to * TOKDEV, TOKDEV), TOKDEV)

    def home(i):
        return remote(
            pieces.at[0, :, home_rows((head + i) % NH), :], hrecv.at[0, head],
            hb_send.at[0, i], hb_recv.at[0, i], at_head(i),
        )

    def home_arrival(i):
        ref = hrecv.at[0, (head + NH - i) % NH]
        return remote(ref, ref, hb_send.at[0, i], hb_recv.at[0, i], at_head(i))

    def home_down(i):
        to = (head + i) % NH
        return remote(
            pieces.at[1, :, home_rows(to), :], hrecv.at[1, head],
            hb_send.at[1, i], hb_recv.at[1, i], (jnp.maximum(z - 1, 0) * NY + y, to),
        )

    def home_down_arrival(i):
        ref = hrecv.at[1, (head + NH - i) % NH]
        return remote(ref, ref, hb_send.at[1, i], hb_recv.at[1, i], at_head(i))

    def leave(at):
        pieces[at, 0] = (total[0] * SCALE).astype(BF16)
        pieces[at, 1] = total[1].astype(BF16)

    def at_level(level, fn, *args):
        pl.when(z >= level)(lambda: fn(*args))

    backward(4, 12, 4)
    grad_y_start(3, 4)
    at_level(3, backward, 3, 8, 4)
    grad_y_start(2)
    lse_step(0)
    at_level(2, backward, 2, 4, 4)
    grad_y_start(1)
    at_level(1, backward, 1, 0, 4)
    grad_y_start(0)
    grad_y_start(3, 0)
    reduce_level(4)
    lse_step(1)
    backward(0, OWN, 1)
    query_gradient(OWN, 1, True)
    reduce_level(3)
    lse_step(2)
    query_gradient(12, 4, False)
    at_level(3, query_gradient, 8, 4, False)
    lse_step(3)
    reduce_level(2)
    at_level(2, query_gradient, 4, 4, False)
    at_level(1, query_gradient, 0, 4, False)
    for h in range(HG):
        cols = slice(h * D, (h + 1) * D)
        att_ref[:, cols] = ot[:, cols].T.astype(BF16)
        gq_ref[:, cols] = (dqt[:, cols] * SCALE).T.astype(BF16)

    @pl.when(z >= 1)
    def _():
        column_sum(1)
        leave(1)
        for i in range(NH):
            home_down(i).start()

    total[...] = wide(part, OWN)
    for i in range(1, NY):
        other = (y + i) % NY

        @pl.when(other > y)
        def _(other=other):
            grad_y_arrival(3, other)
            total[...] += wide(yrecv, 3, other)

    pl.when(z < NZ - 2)(lambda: from_z(2))
    leave(0)
    for i in range(1, NH):
        home(i).start()
    hrecv[0, head] = pieces[0, :, home_rows(head), :]

    lse_step(4)
    lane = lax.broadcasted_iota(jnp.int32, (HG, TOK), 1) // 4
    owned = jnp.zeros((HG, TOK), F32)
    for d in range(NZ * NY):
        moved = pltpu.roll(lgat[d // NY, d % NY], ((d - ctx) * 4) % TOK, 1)
        owned = jnp.where(lane == d, moved, owned)
    lse_ref[...] = owned

    for i in range(1, NH):
        head_copy(i).wait_send()
    for hop in range(1, 5):

        @pl.when(chain_goes(hop))
        def _(hop=hop):
            chain_copy(hop).wait_send()

        if hop > 1:

            @pl.when(z >= hop)
            def _(hop=hop):
                grad_z(hop).wait_send()

    for level in range(5):
        for i in range(1, NY):

            @pl.when(spread_goes(level, i))
            def _(level=level, i=i):
                spread_copy(level, i).wait_send()

    for g in range(4):
        for i in range(1, NY):

            @pl.when(grad_y_goes(g, i))
            def _(g=g, i=i):
                grad_y(g, i).wait_send()

    for i in range(1, NY):
        lse_y(i).wait_send()
    for step in range(4):
        lse_up(step).wait_send()
    for step in range(3):
        lse_down(step).wait_send()

    @pl.when(z == NZ - 1)
    def _():
        hrecv[1] = jnp.zeros((NH, 2, TOKDEV, D), BF16)

    @pl.when(z < NZ - 1)
    def _():
        for i in range(NH):
            home_down_arrival(i).wait_recv()

    for i in range(1, NH):
        home_arrival(i).wait_recv()
    for h in range(NH):
        cols = slice(h * D, (h + 1) * D)
        both = wide(hrecv, 0, h) + wide(hrecv, 1, h)
        gk_ref[:, cols] = both[0].astype(BF16)
        gv_ref[:, cols] = both[1].astype(BF16)

    @pl.when(z >= 1)
    def _():
        for i in range(NH):
            home_down(i).wait_send()

    for i in range(1, NH):
        home(i).wait_send()


def deliver(*refs):
    sem = refs[-1]
    copies = [pltpu.make_async_copy(refs[i], refs[5 + i], sem.at[i]) for i in range(5)]
    for copy in copies:
        copy.start()
    for copy in copies:
        copy.wait()


def body(queries, key_rows, value_rows, grad_out, doc_ids, block_owner):
    vmem = pl.BlockSpec(memory_space=pltpu.VMEM)
    hbm = pl.BlockSpec(memory_space=pltpu.HBM)
    dma = pltpu.SemaphoreType.DMA
    keys = 17 * TOK
    shapes = (
        jax.ShapeDtypeStruct((TOK, ROWS), BF16),
        jax.ShapeDtypeStruct((HG, TOK), F32),
        jax.ShapeDtypeStruct((TOK, ROWS), BF16),
        jax.ShapeDtypeStruct((TOKDEV, NH * D), BF16),
        jax.ShapeDtypeStruct((TOKDEV, NH * D), BF16),
    )
    outs = pl.pallas_call(
        kernel,
        out_shape=shapes,
        in_specs=[hbm] * 6,
        out_specs=(vmem,) * 5,
        scratch_shapes=[
            pltpu.VMEM((TOK, ROWS), BF16),
            pltpu.VMEM((TOK, ROWS), BF16),
            pltpu.VMEM((TOKDEV, NH * D), BF16),
            pltpu.VMEM((TOKDEV, NH * D), BF16),
            pltpu.VMEM((32, TOK), jnp.int32),
            pltpu.VMEM((32, 32), jnp.int32),
            pltpu.VMEM((D, ROWS), BF16),
            pltpu.VMEM((D, ROWS), BF16),
            pltpu.VMEM((ROWS, D), BF16),
            pltpu.VMEM((ROWS, D), BF16),
            pltpu.VMEM((17, 2, TOK, D), BF16),
            pltpu.VMEM((NH, 2, TOKDEV, D), BF16),
            pltpu.VMEM((keys, ROWS), BF16),
            pltpu.VMEM((keys, ROWS), F32),
            pltpu.VMEM((keys, ROWS), BF16),
            pltpu.VMEM((D, keys), BF16),
            pltpu.VMEM((D, 4 * TOK), BF16),
            pltpu.VMEM((D, ROWS), F32),
            pltpu.VMEM((D, ROWS), F32),
            pltpu.VMEM((1, ROWS), F32),
            pltpu.VMEM((1, ROWS), F32),
            pltpu.VMEM((8, ROWS), F32),
            pltpu.VMEM((1, ROWS), F32),
            pltpu.VMEM((17, 2, TOK, D), BF16),
            pltpu.VMEM((4, NY, 2, TOK, D), BF16),
            pltpu.VMEM((3, 2, TOK, D), BF16),
            pltpu.VMEM((3, 2, TOK, D), BF16),
            pltpu.VMEM((2, TOK, D), F32),
            pltpu.VMEM((2, 2, TOK, D), BF16),
            pltpu.VMEM((2, NH, 2, TOKDEV, D), BF16),
            pltpu.VMEM((HG, TOK), F32),
            pltpu.VMEM((NZ, NY, HG, TOK), F32),
            dma((6,)),
            dma((NH,)), dma((NH,)),
            dma((4,)), dma((15,)), dma((17,)),
            dma((12,)), dma((16,)), dma((3,)), dma((3,)),
            dma((2, NH)), dma((2, NH)),
            dma((NY,)), dma((NY,)), dma((NZ,)), dma((NZ,)),
        ],
        compiler_params=pltpu.CompilerParams(
            collective_id=0, has_side_effects=True, vmem_limit_bytes=60 * 1024 * 1024
        ),
        name="packed_attention",
    )(queries, key_rows, value_rows, grad_out, doc_ids.reshape(32, TOK), block_owner)
    return pl.pallas_call(
        deliver,
        out_shape=shapes,
        in_specs=[vmem] * 5,
        out_specs=(hbm,) * 5,
        scratch_shapes=[dma((5,))],
        name="deliver",
    )(*outs)


def solution(mesh):
    return jax.shard_map(
        body,
        mesh=mesh,
        in_specs=(
            P("ctx", "head"), P(("ctx", "head"), None), P(("ctx", "head"), None),
            P("ctx", "head"), P(), P(),
        ),
        out_specs=(
            P("ctx", "head"), P("head", "ctx"), P("ctx", "head"),
            P(("ctx", "head"), None), P(("ctx", "head"), None),
        ),
        check_vma=False,
    )
```

time: 69.9 us -> 60.4 us (0.86)
  the two profiles are of different devices: /device:TPU:65 before, /device:TPU:57 now
where the time goes in v2:
time: 60.4 us; the launch traced here: 60.3 us
  Pallas kernels  59.6 us (99%)
  between operations  0.64 us (1%)
    pallas_call x1, Pallas kernels, body(): pl.pallas_call(kernel, out_shape=shapes, in_specs=[hbm] * 6, out_specs=(v...  57.7 us
    pallas_call x1, Pallas kernels, body(): pl.pallas_call(deliver, out_shape=shapes, in_specs=[vmem] * 5, out_specs=...  1.9 us

profile of v2, /device:TPU:57, one launch (start us, length us, event | category | flops | bytes accessed | tf_op | source)
XLA Modules:
  0.0 60.3 jit_solution(12693955292384501054)
XLA Ops:
  0.6 57.7 %packed_attention.1 = (bf16[128,1024]{1,0:T(8,128)(2,1)}, f32[8,128]{1,0:T(8,128)}, bf16[128,1024]{1,0:T(8,128)(2,1)}, bf16[16,1024]{1,0:T(8,128)(2,1)}, bf16[16,1024]{1,0:T(8,128)(2,1)}) custom-call(bf16[128,1024]{1,0:T(8,128)(2,1)} %q_hbm.1, bf16[16,1024]{1,0:T(8,128)(2,1)} %k_hbm.1, bf16[16,1024]{1,0:T(8,128)(2,1)} %v_hbm.1, bf16[128,1024]{1,0:T(8,128)(2,1)} %g_hbm.1, ...), custom_call_target="tpu_custom_call" | custom-call | tf_op jit(solution)/shard_map/packed_attention/pallas_call | solution.py:600
  58.4 1.9 %deliver.1 = (bf16[128,1024]{1,0:T(8,128)(2,1)}, f32[8,128]{1,0:T(8,128)}, bf16[128,1024]{1,0:T(8,128)(2,1)}, bf16[16,1024]{1,0:T(8,128)(2,1)}, bf16[16,1024]{1,0:T(8,128)(2,1)}) custom-call(bf16[128,1024]{1,0:T(8,128)(2,1)} %get-tuple-element.10.refs_0_, f32[8,128]{1,0:T(8,128)} %get-tuple-element.11.refs_1_, bf16[128,1024]{1,0:T(8,128)(2,1)} %get-tuple-element.12.refs_2_, ...), custom_call_target="tpu_custom_call" | custom-call | tf_op jit(solution)/shard_map/deliver/pallas_call | solution.py:650

commit v3 on v2

--- a/solution.py
+++ b/solution.py
@@ -1,5 +1,3 @@
-import functools
-
 import jax
 import jax.numpy as jnp
 from jax import lax
@@ -32,8 +30,9 @@
 
 def kernel(
     q_hbm, k_hbm, v_hbm, g_hbm, doc_hbm, owner_hbm,
-    att_ref, lse_ref, gq_ref, gk_ref, gv_ref,
+    att_hbm, lse_hbm, gq_hbm, gk_hbm, gv_hbm,
     q_in, g_in, k_ref, v_ref, doc_ref, owner_ref,
+    att_ref, lse_ref, gq_ref, gk_ref, gv_ref, store_sem,
     qt, gt, qs, gs, kv, stage, pbuf, dpb, dsb, kt, tr, ot, dqt, mrun, lrun, mgrp, delta,
     part, yrecv, zrecv, zsend, total, pieces, hrecv, lown, lgat,
     load_sem, ha_send, ha_recv, kz_send, ky_send, kv_recv,
@@ -56,6 +55,16 @@
     for load in loads:
         load.start()
 
+    stores = [
+        pltpu.make_async_copy(src, dst, store_sem.at[i])
+        for i, (src, dst) in enumerate(
+            (
+                (att_ref, att_hbm), (gq_ref, gq_hbm), (lse_ref, lse_hbm),
+                (gk_ref, gk_hbm), (gv_ref, gv_hbm),
+            )
+        )
+    ]
+
     def at_head(i):
         return (ctx, (head + i) % NH)
 
@@ -70,7 +79,7 @@
         pl.semaphore_signal(barrier, inc=1, device_id=at_head(i), device_id_type=MESH)
     for i in range(1, NY):
         pl.semaphore_signal(barrier, inc=1, device_id=at_y(i), device_id_type=MESH)
-    for i in (1, NZ - 1):
+    for i in (1, 2, 4, 6, 7):
         pl.semaphore_signal(barrier, inc=1, device_id=at_z(i), device_id_type=MESH)
 
     loads[0].wait()
@@ -78,7 +87,7 @@
     for h in range(NH):
         stage[h, 0] = k_ref[:, h * D : (h + 1) * D]
         stage[h, 1] = v_ref[:, h * D : (h + 1) * D]
-    pl.semaphore_wait(barrier, NH + NY)
+    pl.semaphore_wait(barrier, NH + NY + 3)
 
     def remote(src, dst, ssem, rsem, to):
         return pltpu.make_async_remote_copy(
@@ -121,19 +130,19 @@
     for i in range(1, NH):
         head_arrival(i).wait_recv()
 
-    def chain_copy(hop):
-        src = kv.at[OWN] if hop == 1 else kv.at[4 * (hop - 2) + y]
-        dst = kv.at[4 * (hop - 1) + y]
-        to = (jnp.minimum(z + 1, NZ - 1) * NY + y, head)
-        return remote(src, dst, kz_send.at[hop - 1], kv_recv.at[4 * (hop - 1) + y], to)
-
-    def chain_goes(hop):
-        return (z < NZ - 1) & (z >= hop - 1)
-
-    def chain_start(hop):
-        @pl.when(chain_goes(hop))
-        def _():
-            chain_copy(hop).start()
+    def level_copy(level):
+        src = kv.at[4 + y] if level == 3 else kv.at[OWN]
+        slot = 4 * (level - 1) + y
+        step = 1 if level == 3 else level
+        return remote(src, kv.at[slot], kz_send.at[level - 1], kv_recv.at[slot], at_z(step))
+
+    def level_goes(level):
+        if level == 3:
+            return (z >= 2) & (z < NZ - 1)
+        return z < NZ - level
+
+    def level_start(level):
+        pl.when(level_goes(level))(lambda: level_copy(level).start())
 
     def spread_copy(level, i):
         src = kv.at[OWN] if level == 0 else kv.at[4 * (level - 1) + y]
@@ -157,7 +166,8 @@
     def slot_arrival(slot):
         remote(kv.at[slot], kv.at[slot], kz_send.at[0], kv_recv.at[slot], at_y(1)).wait_recv()
 
-    chain_start(1)
+    for level in (1, 2, 4):
+        level_start(level)
     spread_start(0)
 
     docs = doc_ref[...]
@@ -229,8 +239,8 @@
         def _():
             slot_arrival(4 * (level - 1) + y)
 
-        if level < 4:
-            chain_start(level + 1)
+        if level == 2:
+            level_start(3)
         spread_start(level)
 
     def await_level(level):
@@ -242,22 +252,12 @@
     forward(0, OWN, 1, [ctx * TOK], True)
     pass_on(1)
     pass_on(2)
-    for level in (1, 2, 3):
-        await_level(level)
-        if level < 3:
-            halfway = functools.partial(pass_on, level + 2)
-
-            @pl.when(z < level)
-            def _(halfway=halfway):
-                halfway()
-
-        else:
-            halfway = None
-
-        @pl.when(z >= level)
-        def _(level=level, halfway=halfway):
-            forward(level, 4 * (level - 1), 4, level_bases(level), False, halfway)
-
+    await_level(1)
+    pass_on(4)
+    pl.when(z < 1)(lambda: pass_on(3))
+    pl.when(z >= 1)(lambda: forward(1, 0, 4, level_bases(1), False, lambda: pass_on(3)))
+    await_level(2)
+    pl.when(z >= 2)(lambda: forward(2, 4, 4, level_bases(2), False))
     for i in range(1, NY):
         other = (y + i) % NY
 
@@ -266,6 +266,8 @@
             slot_arrival(12 + other)
 
     forward(4, 12, 4, mix_bases, False)
+    await_level(3)
+    pl.when(z >= 3)(lambda: forward(3, 8, 4, level_bases(3), False))
 
     def finish(c):
         cols = chunk_of(c)
@@ -462,28 +464,31 @@
     grad_y_start(3, 4)
     at_level(3, backward, 3, 8, 4)
     grad_y_start(2)
-    lse_step(0)
     at_level(2, backward, 2, 4, 4)
     grad_y_start(1)
     at_level(1, backward, 1, 0, 4)
     grad_y_start(0)
     grad_y_start(3, 0)
+    lse_step(0)
     reduce_level(4)
-    lse_step(1)
     backward(0, OWN, 1)
     query_gradient(OWN, 1, True)
+    query_gradient(12, 4, False)
     reduce_level(3)
-    lse_step(2)
-    query_gradient(12, 4, False)
+    lse_step(1)
     at_level(3, query_gradient, 8, 4, False)
-    lse_step(3)
-    reduce_level(2)
-    at_level(2, query_gradient, 4, 4, False)
-    at_level(1, query_gradient, 0, 4, False)
     for h in range(HG):
         cols = slice(h * D, (h + 1) * D)
         att_ref[:, cols] = ot[:, cols].T.astype(BF16)
+    stores[0].start()
+    at_level(2, query_gradient, 4, 4, False)
+    at_level(1, query_gradient, 0, 4, False)
+    reduce_level(2)
+    lse_step(2)
+    for h in range(HG):
+        cols = slice(h * D, (h + 1) * D)
         gq_ref[:, cols] = (dqt[:, cols] * SCALE).T.astype(BF16)
+    stores[1].start()
 
     @pl.when(z >= 1)
     def _():
@@ -492,6 +497,7 @@
         for i in range(NH):
             home_down(i).start()
 
+    lse_step(3)
     total[...] = wide(part, OWN)
     for i in range(1, NY):
         other = (y + i) % NY
@@ -514,14 +520,15 @@
         moved = pltpu.roll(lgat[d // NY, d % NY], ((d - ctx) * 4) % TOK, 1)
         owned = jnp.where(lane == d, moved, owned)
     lse_ref[...] = owned
+    stores[2].start()
 
     for i in range(1, NH):
         head_copy(i).wait_send()
     for hop in range(1, 5):
 
-        @pl.when(chain_goes(hop))
+        @pl.when(level_goes(hop))
         def _(hop=hop):
-            chain_copy(hop).wait_send()
+            level_copy(hop).wait_send()
 
         if hop > 1:
 
@@ -566,6 +573,8 @@
         both = wide(hrecv, 0, h) + wide(hrecv, 1, h)
         gk_ref[:, cols] = both[0].astype(BF16)
         gv_ref[:, cols] = both[1].astype(BF16)
+    stores[3].start()
+    stores[4].start()
 
     @pl.when(z >= 1)
     def _():
@@ -574,6 +583,8 @@
 
     for i in range(1, NH):
         home(i).wait_send()
+    for store in stores:
+        store.wait()
 
 
 def deliver(*refs):
@@ -586,7 +597,6 @@
 
 
 def body(queries, key_rows, value_rows, grad_out, doc_ids, block_owner):
-    vmem = pl.BlockSpec(memory_space=pltpu.VMEM)
     hbm = pl.BlockSpec(memory_space=pltpu.HBM)
     dma = pltpu.SemaphoreType.DMA
     keys = 17 * TOK
@@ -601,7 +611,7 @@
         kernel,
         out_shape=shapes,
         in_specs=[hbm] * 6,
-        out_specs=(vmem,) * 5,
+        out_specs=(hbm,) * 5,
         scratch_shapes=[
             pltpu.VMEM((TOK, ROWS), BF16),
             pltpu.VMEM((TOK, ROWS), BF16),
@@ -609,6 +619,12 @@
             pltpu.VMEM((TOKDEV, NH * D), BF16),
             pltpu.VMEM((32, TOK), jnp.int32),
             pltpu.VMEM((32, 32), jnp.int32),
+            pltpu.VMEM((TOK, ROWS), BF16),
+            pltpu.VMEM((HG, TOK), F32),
+            pltpu.VMEM((TOK, ROWS), BF16),
+            pltpu.VMEM((TOKDEV, NH * D), BF16),
+            pltpu.VMEM((TOKDEV, NH * D), BF16),
+            dma((5,)),
             pltpu.VMEM((D, ROWS), BF16),
             pltpu.VMEM((D, ROWS), BF16),
             pltpu.VMEM((ROWS, D), BF16),
@@ -650,7 +666,7 @@
     return pl.pallas_call(
         deliver,
         out_shape=shapes,
-        in_specs=[vmem] * 5,
+        in_specs=[pl.BlockSpec(memory_space=pltpu.VMEM)] * 5,
         out_specs=(hbm,) * 5,
         scratch_shapes=[dma((5,))],
         name="deliver",

time: 60.4 us -> 58 us (0.960)
  Pallas kernels: 59.6 us -> 57.3 us
    pallas_call x2, Pallas kernels: 59.6 us -> 57.3 us  [the longest x1 55.4 us: body(): pl.pallas_call(kernel, out_shape=shapes, in_specs=[hbm] * 6, out_specs=(h...]
where the time goes in v3:
time: 58 us; the launch traced here: 57.9 us
  Pallas kernels  57.3 us (99%)
  between operations  0.64 us (1%)
    pallas_call x1, Pallas kernels, body(): pl.pallas_call(kernel, out_shape=shapes, in_specs=[hbm] * 6, out_specs=(h...  55.4 us
    pallas_call x1, Pallas kernels, body(): pl.pallas_call(deliver, out_shape=shapes, in_specs=[pl.BlockSpec(memory_s...  1.9 us

profile of v3, /device:TPU:57, one launch (start us, length us, event | category | flops | bytes accessed | tf_op | source)
XLA Modules:
  0.0 57.9 jit_solution(14096547922379312156)
XLA Ops:
  0.6 55.4 %packed_attention.1 = (bf16[128,1024]{1,0:T(8,128)(2,1)}, f32[8,128]{1,0:T(8,128)}, bf16[128,1024]{1,0:T(8,128)(2,1)}, bf16[16,1024]{1,0:T(8,128)(2,1)}, bf16[16,1024]{1,0:T(8,128)(2,1)}) custom-call(bf16[128,1024]{1,0:T(8,128)(2,1)} %q_hbm.1, bf16[16,1024]{1,0:T(8,128)(2,1)} %k_hbm.1, bf16[16,1024]{1,0:T(8,128)(2,1)} %v_hbm.1, bf16[128,1024]{1,0:T(8,128)(2,1)} %g_hbm.1, ...), custom_call_target="tpu_custom_call" | custom-call | tf_op jit(solution)/shard_map/packed_attention/pallas_call | solution.py:610
  56.0 1.9 %deliver.1 = (bf16[128,1024]{1,0:T(8,128)(2,1)}, f32[8,128]{1,0:T(8,128)}, bf16[128,1024]{1,0:T(8,128)(2,1)}, bf16[16,1024]{1,0:T(8,128)(2,1)}, bf16[16,1024]{1,0:T(8,128)(2,1)}) custom-call(bf16[128,1024]{1,0:T(8,128)(2,1)} %get-tuple-element.10.refs_0_, f32[8,128]{1,0:T(8,128)} %get-tuple-element.11.refs_1_, bf16[128,1024]{1,0:T(8,128)(2,1)} %get-tuple-element.12.refs_2_, ...), custom_call_target="tpu_custom_call" | custom-call | tf_op jit(solution)/shard_map/deliver/pallas_call | solution.py:666

commit v4 on v3

v4 whole, which is shorter than its diff:
```python
import jax
import jax.numpy as jnp
from jax import lax
from jax.experimental import pallas as pl
from jax.experimental.pallas import tpu as pltpu
from jax.sharding import PartitionSpec as P

D = 128
TOK = 128
HG = 8
ROWS = HG * TOK
CHUNK = 256
NCHUNK = ROWS // CHUNK
NZ, NY = 8, 4
NH = 8
TOKDEV = 16
OWN = 16
LOG2E = 1.4426950408889634
LN2 = 0.6931471805599453
NEG = -1e30
SCALE = D**-0.5
F32 = jnp.float32
BF16 = jnp.bfloat16
MESH = pl.DeviceIdType.MESH


def dot(a, b):
    return jnp.dot(a, b, preferred_element_type=F32)


def kernel(
    q_hbm, k_hbm, v_hbm, g_hbm, doc_hbm, owner_hbm,
    att_ref, lse_ref, gq_ref, gk_ref, gv_ref,
    q_in, g_in, k_ref, v_ref, doc_ref, owner_ref,
    qt, gt, qs, gs, kv, stage, pbuf, dpb, dsb, ot, dqt, mrun, lrun, mgrp, delta,
    part, yrecv, total, pieces, hrecv, gathered, lown, lgat,
    load_sem, ha_send, ha_recv, kz_send, ky_send, kv_recv,
    gy_send, gy_recv, hb_send, hb_recv, ly_send, ly_recv, lz_send, lz_recv,
):
    ctx = lax.axis_index("ctx")
    head = lax.axis_index("head")
    z = ctx // NY
    y = ctx % NY

    loads = [
        pltpu.make_async_copy(src, dst, load_sem.at[i])
        for i, (src, dst) in enumerate(
            (
                (k_hbm, k_ref), (v_hbm, v_ref), (q_hbm, q_in), (g_hbm, g_in),
                (doc_hbm, doc_ref), (owner_hbm, owner_ref),
            )
        )
    ]
    for load in loads:
        load.start()

    def at_head(i):
        return (ctx, (head + i) % NH)

    def at_y(i):
        return (z * NY + (y + i) % NY, head)

    def at_z(i):
        return (((z + i) % NZ) * NY + y, head)

    barrier = pltpu.get_barrier_semaphore()
    for i in range(1, NH):
        pl.semaphore_signal(barrier, inc=1, device_id=at_head(i), device_id_type=MESH)
    for i in range(1, NY):
        pl.semaphore_signal(barrier, inc=1, device_id=at_y(i), device_id_type=MESH)
    for i in (1, 2, 4):

        @pl.when(z >= i)
        def _(i=i):
            pl.semaphore_signal(barrier, inc=1, device_id=at_z(NZ - i), device_id_type=MESH)


    for i in (5, 6, 7):

        @pl.when(z < NZ - i)
        def _(i=i):
            pl.semaphore_signal(barrier, inc=1, device_id=at_z(i), device_id_type=MESH)

    loads[0].wait()
    loads[1].wait()
    for h in range(NH):
        stage[h, 0] = k_ref[:, h * D : (h + 1) * D]
        stage[h, 1] = v_ref[:, h * D : (h + 1) * D]
    above = sum((z < NZ - i).astype(jnp.int32) for i in (1, 2, 4))
    below = sum((z >= i).astype(jnp.int32) for i in (5, 6, 7))
    pl.semaphore_wait(barrier, NH + NY - 2 + above + below)

    def remote(src, dst, ssem, rsem, to):
        return pltpu.make_async_remote_copy(
            src_ref=src, dst_ref=dst, send_sem=ssem, recv_sem=rsem, device_id=to, device_id_type=MESH
        )

    def head_copy(i):
        to = (head + i) % NH
        rows = pl.ds(pl.multiple_of(head * TOKDEV, TOKDEV), TOKDEV)
        return remote(
            stage.at[to], kv.at[OWN, :, rows, :], ha_send.at[i], ha_recv.at[i], at_head(i)
        )

    def head_arrival(i):
        rows = pl.ds(pl.multiple_of(((head + NH - i) % NH) * TOKDEV, TOKDEV), TOKDEV)
        return remote(stage.at[0], kv.at[OWN, :, rows, :], ha_send.at[i], ha_recv.at[i], at_head(i))

    for i in range(1, NH):
        head_copy(i).start()
    kv[OWN, :, pl.ds(pl.multiple_of(head * TOKDEV, TOKDEV), TOKDEV), :] = stage[head]

    for load in loads[2:]:
        load.wait()
    for h in range(HG):
        cols = slice(h * D, (h + 1) * D)
        qh, gh = q_in[:, cols], g_in[:, cols]
        qs[cols, :] = qh
        gs[cols, :] = gh
        qt[:, cols] = qh.T
        gt[:, cols] = gh.T

    @pl.when(z < 4)
    def _():
        for j in range(NY):

            @pl.when(y <= j)
            def _(j=j):
                kv[12 + j] = jnp.zeros((2, TOK, D), BF16)

    for i in range(1, NH):
        head_arrival(i).wait_recv()

    def level_copy(level, half):
        src = kv.at[4 + y, half] if level == 3 else kv.at[OWN, half]
        slot = 4 * (level - 1) + y
        step = 1 if level == 3 else level
        return remote(
            src, kv.at[slot, half], kz_send.at[half, level - 1], kv_recv.at[half, slot], at_z(step)
        )

    def level_goes(level):
        if level == 3:
            return (z >= 2) & (z < NZ - 1)
        return z < NZ - level

    def level_start(level, half):
        pl.when(level_goes(level))(lambda: level_copy(level, half).start())

    def spread_copy(level, half, i):
        src = kv.at[OWN, half] if level == 0 else kv.at[4 * (level - 1) + y, half]
        slot = 12 + y if level in (0, 4) else 4 * (level - 1) + y
        return remote(
            src, kv.at[slot, half], ky_send.at[half, 3 * level + i - 1], kv_recv.at[half, slot], at_y(i)
        )

    def spread_goes(level, i):
        if level == 0:
            return (y + i) < NY
        if level == 4:
            return (z >= 4) & ((y + i) >= NY)
        return z >= level

    def spread_start(level, half):
        for i in range(1, NY):
            pl.when(spread_goes(level, i))(lambda i=i: spread_copy(level, half, i).start())

    def slot_arrival(slot, half):
        ref = kv.at[slot, half]
        remote(ref, ref, kz_send.at[0, 0], kv_recv.at[half, slot], at_y(1)).wait_recv()

    for half in range(2):
        for level in (1, 2, 4):
            level_start(level, half)
        spread_start(0, half)

    docs = doc_ref[...]
    mine = doc_ref[pl.ds(ctx, 1), :]
    starts = jnp.zeros((1, TOK), F32)
    for v in range(1, 4):
        below = jnp.where(docs < v, 1.0, 0.0).astype(F32)
        count = jnp.sum(jnp.sum(below, axis=0, keepdims=True), axis=1, keepdims=True)
        starts = jnp.where(mine == v, count, starts)
    starts = jnp.concatenate([starts, starts], axis=1)
    tpos = lax.broadcasted_iota(jnp.int32, (1, TOK), 1).astype(F32)
    tpos = jnp.concatenate([tpos, tpos], axis=1) + (ctx * TOK).astype(F32)

    def positions(bases):
        step = lax.broadcasted_iota(jnp.int32, (TOK, 1), 0).astype(F32)
        return jnp.concatenate([step + b.astype(F32) for b in bases], axis=0)

    def chunk_of(c):
        return slice(c * CHUNK, (c + 1) * CHUNK)

    def score(group, slot0, count, bases, diagonal=False):
        n = count * TOK
        span = slice(slot0 * TOK, slot0 * TOK + n)
        keys = kv[slot0 : slot0 + count, 0].reshape(n, D)
        kpos = positions(bases)

        def step(c):
            cols = chunk_of(c)
            s = dot(keys, qt[:, cols]) * (SCALE * LOG2E)
            allowed = kpos >= starts
            if diagonal:
                allowed = allowed & (kpos <= tpos)
            s = jnp.where(allowed, s, NEG)
            top = jnp.max(s, axis=0, keepdims=True)
            if not diagonal:
                before = mrun[:, cols]
                top = jnp.maximum(before, top)
            p = jnp.exp2(s - top)
            mass = jnp.sum(p, axis=0, keepdims=True)
            if not diagonal:
                mass += lrun[:, cols] * jnp.exp2(before - top)
            pbuf[span, cols] = p.astype(BF16)
            lrun[:, cols] = mass
            mrun[:, cols] = top
            mgrp[group : group + 1, cols] = top

        for c in range(NCHUNK):
            step(c)

    def normalise(group, slot0, count):
        span = slice(slot0 * TOK, (slot0 + count) * TOK)

        def step(c):
            cols = chunk_of(c)
            share = jnp.exp2(mgrp[group : group + 1, cols] - mrun[:, cols]) / lrun[:, cols]
            pbuf[span, cols] = (pbuf[span, cols].astype(F32) * share).astype(BF16)

        for c in range(NCHUNK):
            step(c)
        part[slot0 : slot0 + count, 1] = dot(pbuf[span, :], gs[...]).astype(BF16).reshape(count, TOK, D)

    def with_values(slot0, count, first=False):
        n = count * TOK
        span = slice(slot0 * TOK, slot0 * TOK + n)
        values = kv[slot0 : slot0 + count, 1].reshape(n, D)
        across = values.T

        def step(c):
            cols = chunk_of(c)
            dpb[span, cols] = dot(values, gt[:, cols])
            part_o = dot(across, pbuf[span, cols])
            if first:
                ot[:, cols] = part_o
            else:
                ot[:, cols] += part_o

        for c in range(NCHUNK):
            step(c)

    def level_bases(level):
        return [((z - level) * NY + j) * TOK for j in range(NY)]

    mix_bases = [jnp.where(j < y, z * NY + j, (z - 4) * NY + j) * TOK for j in range(NY)]

    def pass_on(level, half):
        pl.when(z >= level)(lambda: slot_arrival(4 * (level - 1) + y, half))
        if level == 2:
            level_start(3, half)
        spread_start(level, half)

    def await_level(level, half):
        @pl.when(z >= level)
        def _():
            for i in range(1, NY):
                slot_arrival(4 * (level - 1) + (y + i) % NY, half)

    def await_mix(half):
        for i in range(1, NY):
            other = (y + i) % NY
            pl.when((other < y) | (z >= 4))(lambda other=other: slot_arrival(12 + other, half))

    def at_level(level, fn, *args):
        pl.when(z >= level)(lambda: fn(*args))

    score(0, OWN, 1, [ctx * TOK], True)
    pass_on(1, 0)
    pass_on(2, 0)
    pass_on(4, 0)
    pass_on(1, 1)
    await_level(1, 0)
    at_level(1, score, 1, 0, 4, level_bases(1))
    pass_on(3, 0)
    pass_on(2, 1)
    await_level(2, 0)
    at_level(2, score, 2, 4, 4, level_bases(2))
    pass_on(4, 1)
    await_mix(0)
    score(4, 12, 4, mix_bases)
    pass_on(3, 1)
    await_level(3, 0)
    at_level(3, score, 3, 8, 4, level_bases(3))

    def grad_y(g, half, i):
        other = (y + i) % NY
        return remote(
            part.at[4 * g + other, half], yrecv.at[g, y, half], gy_send.at[half, 3 * g + i - 1],
            gy_recv.at[half, 4 * g + y], at_y(i),
        )

    def grad_y_goes(g, i, part_of=None):
        if g < 3:
            return z >= g + 1
        own_level, far_level = (y + i) >= NY, ((y + i) < NY) & (z >= 4)
        return {None: own_level | far_level, 0: own_level, 4: far_level}[part_of]

    def grad_y_start(g, half, part_of=None):
        for i in range(1, NY):
            pl.when(grad_y_goes(g, i, part_of))(lambda i=i: grad_y(g, half, i).start())

    def grad_y_arrival(g, other):
        for half in range(2):
            ref = yrecv.at[g, other, half]
            remote(ref, ref, gy_send.at[0, 0], gy_recv.at[half, 4 * g + other], at_y(1)).wait_recv()

    normalise(4, 12, 4)
    grad_y_start(3, 1, 4)
    at_level(3, normalise, 3, 8, 4)
    grad_y_start(2, 1)
    at_level(2, normalise, 2, 4, 4)
    grad_y_start(1, 1)
    at_level(1, normalise, 1, 0, 4)
    grad_y_start(0, 1)
    grad_y_start(3, 1, 0)
    normalise(0, OWN, 1)

    norm = mrun[...] * LN2 + jnp.log(lrun[...])
    for h in range(HG):
        cols = slice(h * D, (h + 1) * D)
        lown[h : h + 1, :] = norm[:, cols]
    reps = lax.broadcasted_iota(jnp.int32, (32, TOK), 1) // 4 == lax.broadcasted_iota(
        jnp.int32, (32, TOK), 0
    )
    owners = dot(owner_ref[pl.ds(ctx, 1), :].astype(F32), jnp.where(reps, 1.0, 0.0).astype(F32))
    to_col = lax.broadcasted_iota(jnp.int32, (TOK, TOK), 0)
    from_tok = lax.broadcasted_iota(jnp.int32, (TOK, TOK), 1)
    hit = (owners == (to_col // 4).astype(F32)) & (to_col % 4 == from_tok % 4)
    lgat[z, y] = lax.dot_general(
        lown[...],
        jnp.where(hit, 1.0, 0.0).astype(F32),
        (((1,), (1,)), ((), ())),
        precision=lax.Precision.HIGHEST,
        preferred_element_type=F32,
    )

    def lse_y(i):
        return remote(lgat.at[z, y], lgat.at[z, y], ly_send.at[i], ly_recv.at[i], at_y(i))

    def lse_y_arrival(i):
        other = (y + NY - i) % NY
        return remote(lgat.at[z, other], lgat.at[z, other], ly_send.at[i], ly_recv.at[i], at_y(i))

    def lse_z(i):
        return remote(lgat.at[z], lgat.at[z], lz_send.at[i], lz_recv.at[i], at_z(i))

    def lse_z_arrival(i):
        block = lgat.at[(z + NZ - i) % NZ]
        return remote(block, block, lz_send.at[i], lz_recv.at[i], at_z(i))

    def lse_down():
        for i in range(1, NY):
            lse_y_arrival(i).wait_recv()
        for i in range(1, NZ):
            pl.when(z >= NZ - i)(lambda i=i: lse_z(i).start())

    def lse_up():
        for i in range(1, NZ):

            @pl.when(z < NZ - i)
            def _(i=i):
                lse_z_arrival(NZ - i).wait_recv()
                lse_z(i).start()

    for i in range(1, NY):
        lse_y(i).start()

    with_values(OWN, 1, True)
    await_level(1, 1)
    at_level(1, with_values, 0, 4)
    await_level(2, 1)
    at_level(2, with_values, 4, 4)
    await_mix(1)
    with_values(12, 4)
    await_level(3, 1)
    at_level(3, with_values, 8, 4)

    def finish(c):
        cols = chunk_of(c)
        full = ot[:, cols].astype(BF16).astype(F32)
        ot[:, cols] = full
        delta[:, cols] = jnp.sum(gt[:, cols].astype(F32) * full, axis=0, keepdims=True)

    for c in range(NCHUNK):
        finish(c)

    def backward(slot0, count):
        span = slice(slot0 * TOK, (slot0 + count) * TOK)

        def step(c):
            cols = chunk_of(c)
            slope = dpb[span, cols] - delta[:, cols]
            dsb[span, cols] = (pbuf[span, cols].astype(F32) * slope).astype(BF16)

        for c in range(NCHUNK):
            step(c)
        part[slot0 : slot0 + count, 0] = dot(dsb[span, :], qs[...]).astype(BF16).reshape(count, TOK, D)

    def query_gradient(slot0, count, first):
        span = slice(slot0 * TOK, (slot0 + count) * TOK)
        across = kv[slot0 : slot0 + count, 0].reshape(count * TOK, D).T

        def step(c):
            cols = chunk_of(c)
            dq = dot(across, dsb[span, cols])
            if first:
                dqt[:, cols] = dq
            else:
                dqt[:, cols] += dq

        for c in range(NCHUNK):
            step(c)

    def wide(ref, *at):
        return ref[at].astype(F32)

    def column_sum(level):
        g = level - 1
        total[...] = wide(part, 4 * g + y)
        for i in range(1, NY):
            other = (y + i) % NY
            if level == 4:

                @pl.when(other < y)
                def _(other=other):
                    grad_y_arrival(g, other)
                    total[...] += wide(yrecv, g, other)
            else:
                grad_y_arrival(g, other)
                total[...] += wide(yrecv, g, other)

    def home_rows(to):
        return pl.ds(pl.multiple_of(to * TOKDEV, TOKDEV), TOKDEV)

    def home(level, i):
        to = (head + i) % NH
        return remote(
            pieces.at[level, :, home_rows(to), :], hrecv.at[level, head],
            hb_send.at[level, i], hb_recv.at[level, i], (jnp.maximum(z - level, 0) * NY + y, to),
        )

    def home_arrival(level, i):
        ref = hrecv.at[level, (head + NH - i) % NH]
        return remote(ref, ref, hb_send.at[level, i], hb_recv.at[level, i], at_head(1))

    def home_start(level):
        pieces[level, 0] = (total[0] * SCALE).astype(BF16)
        pieces[level, 1] = total[1].astype(BF16)
        for i in range(0 if level else 1, NH):
            home(level, i).start()

    def reduce_level(level):
        @pl.when(z >= level)
        def _():
            column_sum(level)
            home_start(level)

    backward(12, 4)
    grad_y_start(3, 0, 4)
    at_level(3, backward, 8, 4)
    grad_y_start(2, 0)
    at_level(2, backward, 4, 4)
    grad_y_start(1, 0)
    at_level(1, backward, 0, 4)
    grad_y_start(0, 0)
    grad_y_start(3, 0, 0)
    lse_down()
    reduce_level(4)
    backward(OWN, 1)
    query_gradient(OWN, 1, True)
    query_gradient(12, 4, False)
    reduce_level(3)
    at_level(3, query_gradient, 8, 4, False)
    for h in range(HG):
        cols = slice(h * D, (h + 1) * D)
        att_ref[:, cols] = ot[:, cols].T.astype(BF16)
    at_level(2, query_gradient, 4, 4, False)
    at_level(1, query_gradient, 0, 4, False)
    reduce_level(2)
    for h in range(HG):
        cols = slice(h * D, (h + 1) * D)
        gq_ref[:, cols] = (dqt[:, cols] * SCALE).T.astype(BF16)

    reduce_level(1)
    lse_up()
    total[...] = wide(part, OWN)
    for i in range(1, NY):
        other = (y + i) % NY

        @pl.when(other > y)
        def _(other=other):
            grad_y_arrival(3, other)
            total[...] += wide(yrecv, 3, other)

    home_start(0)
    hrecv[0, head] = pieces[0, :, home_rows(head), :]

    for i in range(1, NZ):
        pl.when(z >= i)(lambda i=i: lse_z_arrival(i).wait_recv())
    lane = lax.broadcasted_iota(jnp.int32, (HG, TOK), 1) // 4
    owned = jnp.zeros((HG, TOK), F32)
    for d in range(NZ * NY):
        moved = pltpu.roll(lgat[d // NY, d % NY], ((d - ctx) * 4) % TOK, 1)
        owned = jnp.where(lane == d, moved, owned)
    lse_ref[...] = owned

    for i in range(1, NH):
        head_copy(i).wait_send()
    for hop in range(1, 5):

        @pl.when(level_goes(hop))
        def _(hop=hop):
            for half in range(2):
                level_copy(hop, half).wait_send()

    for level in range(5):
        for i in range(1, NY):

            @pl.when(spread_goes(level, i))
            def _(level=level, i=i):
                for half in range(2):
                    spread_copy(level, half, i).wait_send()

    for g in range(4):
        for i in range(1, NY):

            @pl.when(grad_y_goes(g, i))
            def _(g=g, i=i):
                for half in range(2):
                    grad_y(g, half, i).wait_send()

    for i in range(1, NY):
        lse_y(i).wait_send()
    for i in range(1, NZ):
        lse_z(i).wait_send()

    for i in range(1, NH):
        home_arrival(0, i).wait_recv()
    gathered[...] = wide(hrecv, 0)
    for level in range(1, 5):

        @pl.when(z < NZ - level)
        def _(level=level):
            for i in range(NH):
                home_arrival(level, i).wait_recv()
            gathered[...] += wide(hrecv, level)

    for h in range(NH):
        cols = slice(h * D, (h + 1) * D)
        gk_ref[:, cols] = gathered[h, 0].astype(BF16)
        gv_ref[:, cols] = gathered[h, 1].astype(BF16)

    for level in range(1, 5):

        @pl.when(z >= level)
        def _(level=level):
            for i in range(NH):
                home(level, i).wait_send()

    for i in range(1, NH):
        home(0, i).wait_send()


def deliver(*refs):
    sem = refs[-1]
    copies = [pltpu.make_async_copy(refs[i], refs[5 + i], sem.at[i]) for i in range(5)]
    for copy in copies:
        copy.start()
    for copy in copies:
        copy.wait()


def body(queries, key_rows, value_rows, grad_out, doc_ids, block_owner):
    hbm = pl.BlockSpec(memory_space=pltpu.HBM)
    dma = pltpu.SemaphoreType.DMA
    keys = 17 * TOK
    shapes = (
        jax.ShapeDtypeStruct((TOK, ROWS), BF16),
        jax.ShapeDtypeStruct((HG, TOK), F32),
        jax.ShapeDtypeStruct((TOK, ROWS), BF16),
        jax.ShapeDtypeStruct((TOKDEV, NH * D), BF16),
        jax.ShapeDtypeStruct((TOKDEV, NH * D), BF16),
    )
    arrays = (queries, key_rows, value_rows, grad_out, doc_ids.reshape(32, TOK), block_owner)
    outs = pl.pallas_call(
        kernel,
        out_shape=shapes,
        in_specs=[hbm] * 6,
        out_specs=(pl.BlockSpec(memory_space=pltpu.VMEM),) * 5,
        scratch_shapes=[
            pltpu.VMEM((TOK, ROWS), BF16),
            pltpu.VMEM((TOK, ROWS), BF16),
            pltpu.VMEM((TOKDEV, NH * D), BF16),
            pltpu.VMEM((TOKDEV, NH * D), BF16),
            pltpu.VMEM((32, TOK), jnp.int32),
            pltpu.VMEM((32, 32), jnp.int32),
            pltpu.VMEM((D, ROWS), BF16),
            pltpu.VMEM((D, ROWS), BF16),
            pltpu.VMEM((ROWS, D), BF16),
            pltpu.VMEM((ROWS, D), BF16),
            pltpu.VMEM((17, 2, TOK, D), BF16),
            pltpu.VMEM((NH, 2, TOKDEV, D), BF16),
            pltpu.VMEM((keys, ROWS), BF16),
            pltpu.VMEM((keys, ROWS), F32),
            pltpu.VMEM((keys, ROWS), BF16),
            pltpu.VMEM((D, ROWS), F32),
            pltpu.VMEM((D, ROWS), F32),
            pltpu.VMEM((1, ROWS), F32),
            pltpu.VMEM((1, ROWS), F32),
            pltpu.VMEM((8, ROWS), F32),
            pltpu.VMEM((1, ROWS), F32),
            pltpu.VMEM((17, 2, TOK, D), BF16),
            pltpu.VMEM((4, NY, 2, TOK, D), BF16),
            pltpu.VMEM((2, TOK, D), F32),
            pltpu.VMEM((5, 2, TOK, D), BF16),
            pltpu.VMEM((5, NH, 2, TOKDEV, D), BF16),
            pltpu.VMEM((NH, 2, TOKDEV, D), F32),
            pltpu.VMEM((HG, TOK), F32),
            pltpu.VMEM((NZ, NY, HG, TOK), F32),
            dma((6,)),
            dma((NH,)), dma((NH,)),
            dma((2, 4)), dma((2, 15)), dma((2, 17)),
            dma((2, 12)), dma((2, 16)),
            dma((5, NH)), dma((5, NH)),
            dma((NY,)), dma((NY,)), dma((NZ,)), dma((NZ,)),
        ],
        compiler_params=pltpu.CompilerParams(
            collective_id=0, has_side_effects=True, vmem_limit_bytes=48 * 1024 * 1024
        ),
        name="packed_attention",
    )(*(pltpu.with_memory_space_constraint(a, pltpu.HBM) for a in arrays))
    return pl.pallas_call(
        deliver,
        out_shape=shapes,
        in_specs=[pl.BlockSpec(memory_space=pltpu.VMEM)] * 5,
        out_specs=(hbm,) * 5,
        scratch_shapes=[dma((5,))],
        compiler_params=pltpu.CompilerParams(vmem_limit_bytes=2 * 1024 * 1024),
        name="deliver",
    )(*outs)


def solution(mesh):
    return jax.shard_map(
        body,
        mesh=mesh,
        in_specs=(
            P("ctx", "head"), P(("ctx", "head"), None), P(("ctx", "head"), None),
            P("ctx", "head"), P(), P(),
        ),
        out_specs=(
            P("ctx", "head"), P("head", "ctx"), P("ctx", "head"),
            P(("ctx", "head"), None), P(("ctx", "head"), None),
        ),
        check_vma=False,
    )
```

time: 58 us -> 54.1 us (0.933)
  the two profiles are of different devices: /device:TPU:57 before, /device:TPU:65 now
where the time goes in v4:
time: 54.1 us; the launch traced here: 54 us
  Pallas kernels  53.3 us (99%)
  between operations  0.64 us (1%)
    pallas_call x1, Pallas kernels, body(): pl.pallas_call(kernel, out_shape=shapes, in_specs=[hbm] * 6, out_specs=(p...  52.5 us

profile of v4, /device:TPU:65, one launch (start us, length us, event | category | flops | bytes accessed | tf_op | source)
XLA Modules:
  0.0 54.0 jit_solution(16957318066465852087)
XLA Ops:
  0.6 52.5 %packed_attention.1 = (bf16[128,1024]{1,0:T(8,128)(2,1)S(1)}, f32[8,128]{1,0:T(8,128)S(1)}, bf16[128,1024]{1,0:T(8,128)(2,1)S(1)}, bf16[16,1024]{1,0:T(8,128)(2,1)S(1)}, bf16[16,1024]{1,0:T(8,128)(2,1)S(1)}) custom-call(bf16[128,1024]{1,0:T(8,128)(2,1)} %q_hbm.1, bf16[16,1024]{1,0:T(8,128)(2,1)} %k_hbm.1, bf16[16,1024]{1,0:T(8,128)(2,1)} %v_hbm.1, ...), custom_call_target="tpu_custom_call" | custom-call | tf_op jit(solution)/shard_map/packed_attention/pallas_call | solution.py:597
  53.1 0.8 %deliver.1 = (bf16[128,1024]{1,0:T(8,128)(2,1)}, f32[8,128]{1,0:T(8,128)}, bf16[128,1024]{1,0:T(8,128)(2,1)}, bf16[16,1024]{1,0:T(8,128)(2,1)}, bf16[16,1024]{1,0:T(8,128)(2,1)}) custom-call(bf16[128,1024]{1,0:T(8,128)(2,1)S(1)} %get-tuple-element.10.refs_0_, f32[8,128]{1,0:T(8,128)S(1)} %get-tuple-element.11.refs_1_, ...), custom_call_target="tpu_custom_call" | custom-call | tf_op jit(solution)/shard_map/deliver/pallas_call | solution.py:644

commit v5 on v4

--- a/solution.py
+++ b/solution.py
@@ -365,14 +365,25 @@
             lse_y_arrival(i).wait_recv()
         for i in range(1, NZ):
             pl.when(z >= NZ - i)(lambda i=i: lse_z(i).start())
-
-    def lse_up():
-        for i in range(1, NZ):
-
-            @pl.when(z < NZ - i)
-            def _(i=i):
-                lse_z_arrival(NZ - i).wait_recv()
-                lse_z(i).start()
+        for i in (1, 2, 4):
+            pl.when(z < NZ - i)(lambda i=i: lse_z(i).start())
+
+    relays = {3: (2, 1), 5: (4, 1), 6: (4, 2), 7: (6, 1)}
+
+    def lse_relay(far):
+        back, step = relays[far]
+        block = lgat.at[(z + NZ - back) % NZ]
+        return remote(block, block, lz_send.at[NZ + far], lz_recv.at[far], at_z(step))
+
+    def lse_relay_goes(far):
+        back, step = relays[far]
+        return (z >= back) & (z < NZ - step)
+
+    def lse_pass(*fars):
+        for i in sorted({relays[far][0] for far in fars}):
+            pl.when(z >= i)(lambda i=i: lse_z_arrival(i).wait_recv())
+        for far in fars:
+            pl.when(lse_relay_goes(far))(lambda far=far: lse_relay(far).start())
 
     for i in range(1, NY):
         lse_y(i).start()
@@ -482,6 +493,7 @@
     query_gradient(OWN, 1, True)
     query_gradient(12, 4, False)
     reduce_level(3)
+    lse_pass(3, 5, 6)
     at_level(3, query_gradient, 8, 4, False)
     for h in range(HG):
         cols = slice(h * D, (h + 1) * D)
@@ -489,12 +501,12 @@
     at_level(2, query_gradient, 4, 4, False)
     at_level(1, query_gradient, 0, 4, False)
     reduce_level(2)
+    lse_pass(7)
     for h in range(HG):
         cols = slice(h * D, (h + 1) * D)
         gq_ref[:, cols] = (dqt[:, cols] * SCALE).T.astype(BF16)
 
     reduce_level(1)
-    lse_up()
     total[...] = wide(part, OWN)
     for i in range(1, NY):
         other = (y + i) % NY
@@ -508,7 +520,10 @@
     hrecv[0, head] = pieces[0, :, home_rows(head), :]
 
     for i in range(1, NZ):
-        pl.when(z >= i)(lambda i=i: lse_z_arrival(i).wait_recv())
+        if i in (2, 4, 6):
+            pl.when(z < i)(lambda i=i: lse_z_arrival(i).wait_recv())
+        else:
+            lse_z_arrival(i).wait_recv()
     lane = lax.broadcasted_iota(jnp.int32, (HG, TOK), 1) // 4
     owned = jnp.zeros((HG, TOK), F32)
     for d in range(NZ * NY):
@@ -544,7 +559,11 @@
     for i in range(1, NY):
         lse_y(i).wait_send()
     for i in range(1, NZ):
-        lse_z(i).wait_send()
+        if i in relays:
+            pl.when(z >= NZ - i)(lambda i=i: lse_z(i).wait_send())
+            pl.when(lse_relay_goes(i))(lambda i=i: lse_relay(i).wait_send())
+        else:
+            lse_z(i).wait_send()
 
     for i in range(1, NH):
         home_arrival(0, i).wait_recv()
@@ -634,7 +653,7 @@
             dma((2, 4)), dma((2, 15)), dma((2, 17)),
             dma((2, 12)), dma((2, 16)),
             dma((5, NH)), dma((5, NH)),
-            dma((NY,)), dma((NY,)), dma((NZ,)), dma((NZ,)),
+            dma((NY,)), dma((NY,)), dma((2 * NZ,)), dma((NZ,)),
         ],
         compiler_params=pltpu.CompilerParams(
             collective_id=0, has_side_effects=True, vmem_limit_bytes=48 * 1024 * 1024

time: 54.1 us -> 54.2 us (level)
  no operation moved by 1% of the time
where the time goes in v5:
time: 54.2 us; the launch traced here: 54.1 us
  Pallas kernels  53.4 us (99%)
  between operations  0.64 us (1%)
    pallas_call x1, Pallas kernels, body(): pl.pallas_call(kernel, out_shape=shapes, in_specs=[hbm] * 6, out_specs=(p...  52.6 us

profile of v5, /device:TPU:65, one launch (start us, length us, event | category | flops | bytes accessed | tf_op | source)
XLA Modules:
  0.0 54.1 jit_solution(9218312887703741512)
XLA Ops:
  0.6 52.6 %packed_attention.1 = (bf16[128,1024]{1,0:T(8,128)(2,1)S(1)}, f32[8,128]{1,0:T(8,128)S(1)}, bf16[128,1024]{1,0:T(8,128)(2,1)S(1)}, bf16[16,1024]{1,0:T(8,128)(2,1)S(1)}, bf16[16,1024]{1,0:T(8,128)(2,1)S(1)}) custom-call(bf16[128,1024]{1,0:T(8,128)(2,1)} %q_hbm.1, bf16[16,1024]{1,0:T(8,128)(2,1)} %k_hbm.1, bf16[16,1024]{1,0:T(8,128)(2,1)} %v_hbm.1, ...), custom_call_target="tpu_custom_call" | custom-call | tf_op jit(solution)/shard_map/packed_attention/pallas_call | solution.py:616
  53.2 0.8 %deliver.1 = (bf16[128,1024]{1,0:T(8,128)(2,1)}, f32[8,128]{1,0:T(8,128)}, bf16[128,1024]{1,0:T(8,128)(2,1)}, bf16[16,1024]{1,0:T(8,128)(2,1)}, bf16[16,1024]{1,0:T(8,128)(2,1)}) custom-call(bf16[128,1024]{1,0:T(8,128)(2,1)S(1)} %get-tuple-element.10.refs_0_, f32[8,128]{1,0:T(8,128)S(1)} %get-tuple-element.11.refs_1_, ...), custom_call_target="tpu_custom_call" | custom-call | tf_op jit(solution)/shard_map/deliver/pallas_call | solution.py:663

commit v6 on v4

--- a/solution.py
+++ b/solution.py
@@ -280,10 +280,10 @@
     pass_on(1, 0)
     pass_on(2, 0)
     pass_on(4, 0)
-    pass_on(1, 1)
     await_level(1, 0)
     at_level(1, score, 1, 0, 4, level_bases(1))
     pass_on(3, 0)
+    pass_on(1, 1)
     pass_on(2, 1)
     await_level(2, 0)
     at_level(2, score, 2, 4, 4, level_bases(2))

time: 54.1 us -> 53.8 us (level)
  no operation moved by 1% of the time
where the time goes in v6:
time: 53.8 us; the launch traced here: 53.6 us
  Pallas kernels  53 us (99%)
  between operations  0.64 us (1%)
    pallas_call x1, Pallas kernels, body(): pl.pallas_call(kernel, out_shape=shapes, in_specs=[hbm] * 6, out_specs=(p...  52.1 us

profile of v6, /device:TPU:65, one launch (start us, length us, event | category | flops | bytes accessed | tf_op | source)
XLA Modules:
  0.0 53.6 jit_solution(8179615762461415190)
XLA Ops:
  0.6 52.1 %packed_attention.1 = (bf16[128,1024]{1,0:T(8,128)(2,1)S(1)}, f32[8,128]{1,0:T(8,128)S(1)}, bf16[128,1024]{1,0:T(8,128)(2,1)S(1)}, bf16[16,1024]{1,0:T(8,128)(2,1)S(1)}, bf16[16,1024]{1,0:T(8,128)(2,1)S(1)}) custom-call(bf16[128,1024]{1,0:T(8,128)(2,1)} %q_hbm.1, bf16[16,1024]{1,0:T(8,128)(2,1)} %k_hbm.1, bf16[16,1024]{1,0:T(8,128)(2,1)} %v_hbm.1, ...), custom_call_target="tpu_custom_call" | custom-call | tf_op jit(solution)/shard_map/packed_attention/pallas_call | solution.py:597
  52.8 0.8 %deliver.1 = (bf16[128,1024]{1,0:T(8,128)(2,1)}, f32[8,128]{1,0:T(8,128)}, bf16[128,1024]{1,0:T(8,128)(2,1)}, bf16[16,1024]{1,0:T(8,128)(2,1)}, bf16[16,1024]{1,0:T(8,128)(2,1)}) custom-call(bf16[128,1024]{1,0:T(8,128)(2,1)S(1)} %get-tuple-element.10.refs_0_, f32[8,128]{1,0:T(8,128)S(1)} %get-tuple-element.11.refs_1_, ...), custom_call_target="tpu_custom_call" | custom-call | tf_op jit(solution)/shard_map/deliver/pallas_call | solution.py:644
